TPU v7x, 128 devices: a whole 4x4x4 slice. The times are simulated.
128 devices in a mesh: section: 8 (over z, core), head: 16 (over y, x).
Axes of the slice: x: 4, y: 4, z: 4, core: 2. Of those that a mesh axis runs over, the one named last changes fastest.
Arguments:
- hidden_in: bfloat16 [24576, 2048], P(('section', 'head')), may hold values from -3 to 3
- norm_gain: float32 [2048], replicated, may hold values from 0.1 to 1.9
- w_qkv: bfloat16 [2048, 3, 2048], P(None, None, 'head'), may hold values from -0.5 to 0.5
- w_out: bfloat16 [2048, 2048], P('head'), may hold values from -0.375 to 0.375
- block_lists: int32 [48, 12], P('section'), may hold values from -1 to 47, as said below
Outputs:
- mixed: bfloat16 [24576, 2048], P(('section', 'head'))
Inputs may be any that keep to these rules, and one draw needn't show every extreme that they name: `block_lists`: row b starts with b itself, then holds 1 + b * 11 // 47 - 1 further distinct blocks below b, then -1 in every remaining slot.
All inputs are finite; a program needn't handle non-finite values.
Results may differ from a plain program's by a relative error of at most 0.015.
Values may be sent and summed in bfloat16 or wider, within the bound.
A program may use at most 128 MiB of HBM per device.

v0:
```python
import math

import jax
import jax.numpy as jnp
from jax import lax
from jax.sharding import PartitionSpec as P

D = 2048
HD = 128
BLK = 512


EPS = 1e-05
THETA = 10000.0


def rotate(vectors, cosine, sine):
    half = vectors.shape[-1] // 2
    first = vectors[..., :half]
    second = vectors[..., half:]
    return jnp.concatenate(
        [first * cosine - second * sine, second * cosine + first * sine], axis=-1
    )


def local(hidden_in, norm_gain, w_qkv, w_out, block_lists):
    section_id = lax.axis_index("section")
    width = w_qkv.shape[2]
    heads_here = width // HD
    blocks_here = block_lists.shape[0]
    tok_dev = blocks_here * BLK
    scale = 1.0 / math.sqrt(HD)
    resid = hidden_in.astype(jnp.float32)
    normed = (
        resid * lax.rsqrt(jnp.mean(resid * resid, axis=-1, keepdims=True) + EPS) * norm_gain
    ).astype(jnp.bfloat16)
    flat_weight = w_qkv.reshape(D, 3 * width)
    frequency = THETA ** (-(2.0 * jnp.arange(HD // 2, dtype=jnp.float32)) / HD)
    piece = lax.all_gather(normed, "head", axis=0, tiled=True)
    count = piece.shape[0]
    mixed_rows = jnp.dot(piece, flat_weight, preferred_element_type=jnp.float32).reshape(
        count, 3, heads_here, HD
    )
    positions = (section_id * tok_dev + jnp.arange(count, dtype=jnp.int32)).astype(jnp.float32)
    angle = positions[:, None] * frequency[None, :]
    cosine = jnp.cos(angle)[:, None, :]
    sine = jnp.sin(angle)[:, None, :]
    query_part = rotate(mixed_rows[:, 0], cosine, sine).astype(jnp.bfloat16).reshape(count, width)
    key_part = rotate(mixed_rows[:, 1], cosine, sine).astype(jnp.bfloat16).reshape(count, width)
    value_part = mixed_rows[:, 2].astype(jnp.bfloat16).reshape(count, width)
    section_rows = jnp.concatenate([query_part, key_part, value_part], axis=1)
    query = section_rows[:, :width]
    keys = section_rows[:, width : 2 * width]
    values = section_rows[:, 2 * width :]
    keys_all, values_all = (
        lax.all_gather(keys, "section", axis=0, tiled=True),
        lax.all_gather(values, "section", axis=0, tiled=True),
    )
    count_blocks = block_lists.shape[0]
    query_blocks = query.reshape(count_blocks, BLK, heads_here, HD)
    block_ids = section_id * blocks_here + jnp.arange(count_blocks, dtype=jnp.int32)

    def one_block(carry, item):
        query_block, block_row, block_id = item
        live_slots = jnp.sum((block_row >= 0).astype(jnp.int32))
        query_positions = block_id * BLK + jnp.arange(BLK, dtype=jnp.int32)

        def one_slot(slot, state):
            highest, total, weighted = state
            source = block_row[slot]
            key_block = lax.dynamic_slice_in_dim(keys_all, source * BLK, BLK, 0).reshape(
                BLK, heads_here, HD
            )
            value_block = lax.dynamic_slice_in_dim(values_all, source * BLK, BLK, 0).reshape(
                BLK, heads_here, HD
            )
            scores = (
                jnp.einsum(
                    "qhd,khd->hqk", query_block, key_block, preferred_element_type=jnp.float32
                )
                * scale
            )
            key_positions = source * BLK + jnp.arange(BLK, dtype=jnp.int32)
            scores = jnp.where(
                key_positions[None, None, :] <= query_positions[None, :, None], scores, -jnp.inf
            )
            new_highest = jnp.maximum(highest, jnp.max(scores, axis=-1))
            factor = jnp.exp(highest - new_highest)
            weights = jnp.exp(scores - new_highest[..., None])
            total = total * factor + jnp.sum(weights, axis=-1)
            update = jnp.einsum(
                "hqk,khd->hqd",
                weights.astype(jnp.bfloat16),
                value_block,
                preferred_element_type=jnp.float32,
            )
            weighted = weighted * factor[..., None] + update
            return (new_highest, total, weighted)

        start_state = (
            jnp.full((heads_here, BLK), -jnp.inf, jnp.float32),
            jnp.zeros((heads_here, BLK), jnp.float32),
            jnp.zeros((heads_here, BLK, HD), jnp.float32),
        )
        highest, total, weighted = lax.fori_loop(0, live_slots, one_slot, start_state)
        result = (
            (weighted / total[..., None])
            .transpose(1, 0, 2)
            .reshape(BLK, width)
            .astype(jnp.bfloat16)
        )
        return (carry, result)

    _, results = lax.scan(
        one_block, jnp.zeros((), jnp.int32), (query_blocks, block_lists, block_ids)
    )
    attended = results.reshape(count_blocks * BLK, width)
    regrouped = lax.all_to_all(attended, "head", split_axis=0, concat_axis=1, tiled=True)
    summed = jnp.dot(
        regrouped,
        lax.all_gather(w_out, "head", axis=0, tiled=True),
        preferred_element_type=jnp.float32,
    )
    return (resid + summed).astype(jnp.bfloat16)


def solution(mesh):
    placed = (
        P(("section", "head"), None),
        P(),
        P(None, None, "head"),
        P("head", None),
        P("section", None),
    )
    return jax.shard_map(
        local, mesh=mesh, in_specs=placed, out_specs=P(("section", "head"), None), check_vma=False
    )
```

profile of v0, /device:TPU:97, one launch (start us, length us, event | category | flops | bytes accessed | tf_op | source)
XLA Modules:
  0.0 561.3 jit_solution(7446976114135447886)
XLA Ops:
  6.5 1.5 fusion.20
  8.0 2.3 fusion.22
  11.1 90.2 %all-gather.6.cloned.1.call-done = bf16[3072,2048]{1,0:T(8,128)(2,1)} async-done(((bf16[192,2048]{1,0:T(8,128)(2,1)}), bf16[3072,2048]{1,0:T(8,128)(2,1)}) %all-gather.6.cloned.1.call-update) | async-done | bytes 12582928 | tf_op jit(solution)/shard_map/all_gather | solution.py:39
  101.3 8.1 %fusion.17 = f32[3072,3,128]{0,2,1:T(8,128)S(1)} fusion(bf16[3072,2048]{1,0:T(8,128)(2,1)} %all-gather.6.cloned.1.call-done, bf16[2048,3,128]{0,2,1:T(8,128)(2,1)S(1)} %copy.17), kind=kOutput, calls=%fused_computation.26 | convolution fusion | flops 4831838208 | bytes 18874368 | tf_op jit(solution)/shard_map/dot_general | solution.py:41
  109.3 2.1 copy-done
  112.6 1.5 slice_bitcast_fusion
  114.1 1.5 slice_bitcast_fusion.1
  115.7 3.4 fusion.43
  122.7 29.2 %all-gather.12.cloned.1.call-done = bf16[24576,1,1,128]{0,3,1,2:T(8,128)(2,1)} async-done(((bf16[3072,1,1,128]{0,3,1,2:T(8,128)(2,1)}), bf16[24576,1,1,128]{0,3,1,2:T(8,128)(2,1)}) %all-gather.12.cloned.1.call-update) | async-done | bytes 6291472 | tf_op jit(solution)/shard_map/all_gather | solution.py:57
  151.9 8.5 %copy.21 = bf16[24576,128]{1,0:T(8,128)(2,1)} copy(bf16[24576,128]{0,1:T(8,128)(2,1)} %bitcast.83) | data formatting | bytes 12582912 | tf_op jit(solution)/shard_map/while | solution.py:114
  160.4 34.2 %all-gather.8.cloned.1.call-done = bf16[24576,128]{0,1:T(8,128)(2,1)} async-done(((bf16[3072,128]{0,1:T(8,128)(2,1)}), bf16[24576,128]{0,1:T(8,128)(2,1)}) %all-gather.8.cloned.1.call-update) | async-done | bytes 6291472 | tf_op jit(solution)/shard_map/all_gather | solution.py:56
  194.6 8.7 %copy.20 = bf16[24576,128]{1,0:T(8,128)(2,1)} copy(bf16[24576,128]{0,1:T(8,128)(2,1)} %all-gather.8.cloned.1.call-done) | data formatting | bytes 12582912 | tf_op jit(solution)/shard_map/while | solution.py:114
  203.3 328.3 %while.26 = (s32[]{:T(128)}, bf16[6,512,128]{2,1,0:T(8,128)(2,1)}, s32[6,12]{1,0:T(8,128)}, bf16[6,512,1,128]{3,1,2,0:T(8,128)(2,1)S(1)}, s32[6]{0:T(128)S(1)}, ...) while((s32[]{:T(128)}, bf16[6,512,128]{2,1,0:T(8,128)(2,1)}, ...), condition=%wide.region_7.8_spmd, body=%wide.region_1.7_spmd.sunk | while | flops 136579104 | bytes 5029030 | solution.py:114
  203.3 1.4 fusion.55
  206.1 46.6 %while.27 = (s32[]{:T(128)}, f32[1,512]{1,0:T(1,128)S(1)}, f32[1,512]{1,0:T(1,128)S(1)}, f32[1,512,128]{2,1,0:T(8,128)S(1)}, s32[]{:T(128)}, /*index=5*/s32[12]{...) while((s32[]{:T(128)}, f32[1,512]{1,0:T(1,128)S(1)}, ...), condition=%wide.region_6.6_spmd.clone, body=%wide.region_3.5_spmd.clone.sunk | while | flops 136448000 | bytes 4104441 | solution.py:105
  256.3 51.1 %while.27 = (s32[]{:T(128)}, f32[1,512]{1,0:T(1,128)S(1)}, f32[1,512]{1,0:T(1,128)S(1)}, f32[1,512,128]{2,1,0:T(8,128)S(1)}, s32[]{:T(128)}, /*index=5*/s32[12]{...) while((s32[]{:T(128)}, f32[1,512]{1,0:T(1,128)S(1)}, ...), condition=%wide.region_6.6_spmd.clone, body=%wide.region_3.5_spmd.clone.sunk | while | flops 136448000 | bytes 4104441 | solution.py:105
  308.2 1.4 fusion.55
  311.0 51.1 %while.27 = (s32[]{:T(128)}, f32[1,512]{1,0:T(1,128)S(1)}, f32[1,512]{1,0:T(1,128)S(1)}, f32[1,512,128]{2,1,0:T(8,128)S(1)}, s32[]{:T(128)}, /*index=5*/s32[12]{...) while((s32[]{:T(128)}, f32[1,512]{1,0:T(1,128)S(1)}, ...), condition=%wide.region_6.6_spmd.clone, body=%wide.region_3.5_spmd.clone.sunk | while | flops 136448000 | bytes 4104441 | solution.py:105
  365.7 51.1 %while.27 = (s32[]{:T(128)}, f32[1,512]{1,0:T(1,128)S(1)}, f32[1,512]{1,0:T(1,128)S(1)}, f32[1,512,128]{2,1,0:T(8,128)S(1)}, s32[]{:T(128)}, /*index=5*/s32[12]{...) while((s32[]{:T(128)}, f32[1,512]{1,0:T(1,128)S(1)}, ...), condition=%wide.region_6.6_spmd.clone, body=%wide.region_3.5_spmd.clone.sunk | while | flops 136448000 | bytes 4104441 | solution.py:105
  420.4 51.1 %while.27 = (s32[]{:T(128)}, f32[1,512]{1,0:T(1,128)S(1)}, f32[1,512]{1,0:T(1,128)S(1)}, f32[1,512,128]{2,1,0:T(8,128)S(1)}, s32[]{:T(128)}, /*index=5*/s32[12]{...) while((s32[]{:T(128)}, f32[1,512]{1,0:T(1,128)S(1)}, ...), condition=%wide.region_6.6_spmd.clone, body=%wide.region_3.5_spmd.clone.sunk | while | flops 136448000 | bytes 4104441 | solution.py:105
  475.1 55.6 %while.27 = (s32[]{:T(128)}, f32[1,512]{1,0:T(1,128)S(1)}, f32[1,512]{1,0:T(1,128)S(1)}, f32[1,512,128]{2,1,0:T(8,128)S(1)}, s32[]{:T(128)}, /*index=5*/s32[12]{...) while((s32[]{:T(128)}, f32[1,512]{1,0:T(1,128)S(1)}, ...), condition=%wide.region_6.6_spmd.clone, body=%wide.region_3.5_spmd.clone.sunk | while | flops 136448000 | bytes 4104441 | solution.py:105
  531.6 6.7 %all-to-all-start = ((bf16[16,192,128]{2,1,0:T(8,128)(2,1)}), bf16[16,192,128]{2,1,0:T(8,128)(2,1)S(1)}, u32[]{:S(2)}, u32[]{:S(2)}) async-start(bf16[16,192,128]{2,1,0:T(8,128)(2,1)} %bitcast.15), calls=%async_computation | async-start | bytes 1572864 | tf_op jit(solution)/shard_map/all_to_all | solution.py:118
  538.3 10.4 %all-to-all-done = bf16[16,192,128]{2,1,0:T(8,128)(2,1)S(1)} async-done(((bf16[16,192,128]{2,1,0:T(8,128)(2,1)}), bf16[16,192,128]{2,1,0:T(8,128)(2,1)S(1)}, u32[]{:S(2)}, u32[]{:S(2)}) %all-to-all-start) | async-done | bytes 786464 | tf_op jit(solution)/shard_map/all_to_all | solution.py:118
  548.7 6.1 %fusion.19 = bf16[192,2048]{1,0:T(8,128)(2,1)} fusion(bf16[2048,2048]{1,0:T(8,128)(2,1)} %all-gather.10.cloned.1.call-done, bf16[192,2048]{1,0:T(8,128)(2,1)S(1)} %copy-done.1, bf16[16,192,128]{2,1,0:T(8,128)(2,1)S(1)} %all-to-all-done), kind=kOutput, calls=%fused_computation.29 | convolution fusion | flops 1611792384 | bytes 10747904 | tf_op jit(solution)/shard_map/dot_general | solution.py:119
  (594 shorter events, 238.4 us)
Async XLA Ops:
  6.5 3.8 copy-start.2
  6.5 94.7 %all-gather.6.cloned.1.call-start = ((), (), s32[]{:S(2)}) async-start(), calls=%async_computation.1 | async-start | bytes 13369344 | tf_op jit(solution)/shard_map/all_gather | solution.py:39
  10.3 141.5 %all-gather.12.cloned.1.call-start = ((), (), s32[]{:S(2)}) async-start(), calls=%async_computation.4 | async-start | bytes 7077888 | tf_op jit(solution)/shard_map/all_gather | solution.py:57
  109.3 2.1 copy-start
  112.5 82.0 %all-gather.8.cloned.1.call-start = ((), (), s32[]{:S(2)}) async-start(), calls=%async_computation.2 | async-start | bytes 7077888 | tf_op jit(solution)/shard_map/all_gather | solution.py:56
  120.1 418.2 %all-gather.10.cloned.1.call-start = ((), (), s32[]{:S(2)}) async-start(), calls=%async_computation.3 | async-start | bytes 8912896 | tf_op jit(solution)/shard_map/all_gather | solution.py:121
  531.6 17.1 %copy-start.1 = (bf16[192,2048]{1,0:T(8,128)(2,1)S(1)}, bf16[192,2048]{1,0:T(8,128)(2,1)}, u32[]{:S(2)}) copy-start(bf16[192,2048]{1,0:T(8,128)(2,1)} %param.9) | copy-start | bytes 2359300
  531.6 17.1 %all-to-all-start = ((bf16[16,192,128]{2,1,0:T(8,128)(2,1)}), bf16[16,192,128]{2,1,0:T(8,128)(2,1)S(1)}, u32[]{:S(2)}, u32[]{:S(2)}) async-start(bf16[16,192,128]{2,1,0:T(8,128)(2,1)} %bitcast.15), calls=%async_computation | async-start | bytes 1572864 | tf_op jit(solution)/shard_map/all_to_all | solution.py:118
Sparse Core Ops, SparseCore 0:
  10.4 90.7 all-gather.5
  112.7 39.1 all-gather.11
  153.6 40.9 all-gather.7
  196.6 72.1 all-gather.9
where the time goes:
time: 566 us; the launch traced here: 561 us
  matrix products  181 us (32%)
  waiting for transfers between devices  165 us (29%)
  loops' own time  92.6 us (16%)
  local copies, waits for them, and re-layouts  66.8 us (12%)
  other arithmetic  36.6 us (6%)
  between operations  13.3 us (2%)
  starting transfers between devices  6.8 us (1%)
    all_gather x1, waiting for transfers between devices, local(): piece = lax.all_gather(normed, 'head', axis=0, tiled=True)  90.2 us
    another operation x6, loops' own time, one_block(): lax.fori_loop(0, live_slots, one_slot, start_state)  88.2 us
    dot_general x66, matrix products, one_slot(): jnp.einsum('hqk,khd->hqd', weights.astype(jnp.bfloat16), value_block, pre...  85.5 us
    dot_general x66, matrix products, one_slot(): jnp.einsum('qhd,khd->hqk', query_block, key_block, preferred_element_type...  81.1 us
    dynamic_slice x66, local copies, waits for them, and re-layouts, one_slot(): source = block_row[slot]  36.5 us
    all_gather x1, waiting for transfers between devices, local(): lax.all_gather(keys, 'section', axis=0, tiled=True)  34.2 us
    all_gather x1, waiting for transfers between devices, local(): lax.all_gather(values, 'section', axis=0, tiled=True)  29.2 us
    while x3, local copies, waits for them, and re-layouts, local(): lax.scan(one_block, jnp.zeros((), jnp.int32), (query_blocks, block_lists,...  18 us
  transfers between devices with their start and end apart: 5, of which 4 were waited for; matrix products, arithmetic and copies ran while one was open for 47% of the time, Pallas kernels for 0%

commit v1 on v0

v1 whole, which is shorter than its diff:
```python
import functools
import math

import jax
import jax.numpy as jnp
from jax import lax
from jax.experimental import pallas as pl
from jax.experimental.pallas import tpu as pltpu
from jax.sharding import PartitionSpec as P

D = 2048
HD = 128
BLK = 512
KSEL = 12


EPS = 1e-05
THETA = 10000.0
QSCALE = math.log2(math.e) / math.sqrt(HD)
ROWS = 256


def rotate(vectors, cosine, sine):
    half = vectors.shape[-1] // 2
    first = vectors[..., :half]
    second = vectors[..., half:]
    return jnp.concatenate(
        [first * cosine - second * sine, second * cosine + first * sine], axis=-1
    )


def attention_kernel(lists, q_ref, kv_hbm, o_ref, kv_buf, m_ref, acc_ref, sems):
    blocks = q_ref.shape[0] // BLK

    def live(block):
        count = jnp.int32(0)
        for slot in range(KSEL):
            count += (lists[block, slot] >= 0).astype(jnp.int32)
        return count

    def fetch(block, slot):
        source = jnp.maximum(lists[block, slot], 0)
        start = pl.multiple_of(source * BLK, BLK)
        return pltpu.make_async_copy(
            kv_hbm.at[pl.ds(start, BLK), :],
            kv_buf.at[block % 2, slot],
            sems.at[block % 2, slot],
        )

    def fetch_all(block):
        def one(slot, carry):
            fetch(block, slot).start()
            return carry

        lax.fori_loop(0, live(block), one, 0)

    ones = jnp.ones((BLK, HD), jnp.bfloat16)
    fetch_all(0)

    def one_block(block, carry):
        @pl.when(block + 1 < blocks)
        def _():
            fetch_all(block + 1)

        base = pl.multiple_of(block * BLK, BLK)

        def tile(slot, first):
            keys = kv_buf[block % 2, slot, :, :HD]
            values = jnp.concatenate([kv_buf[block % 2, slot, :, HD:], ones], axis=1)
            for part in range(BLK // ROWS):
                rows = pl.ds(part * ROWS, ROWS)
                query = q_ref[pl.ds(pl.multiple_of(base + part * ROWS, ROWS), ROWS), :]
                scores = lax.dot_general(
                    query, keys, (((1,), (1,)), ((), ())), preferred_element_type=jnp.float32
                )
                if first:
                    row = lax.broadcasted_iota(jnp.int32, (ROWS, BLK), 0) + part * ROWS
                    col = lax.broadcasted_iota(jnp.int32, (ROWS, BLK), 1)
                    scores = jnp.where(col <= row, scores, -jnp.inf)
                peak = jnp.max(scores, axis=1, keepdims=True)
                if not first:
                    old = m_ref[rows, :1]
                    peak = jnp.maximum(peak, old)
                weights = jnp.exp2(scores - peak).astype(jnp.bfloat16)
                update = jnp.dot(weights, values, preferred_element_type=jnp.float32)
                if first:
                    acc_ref[rows, :] = update
                else:
                    acc_ref[rows, :] = acc_ref[rows, :] * jnp.exp2(old - peak) + update
                m_ref[rows, :] = jnp.broadcast_to(peak, (ROWS, HD))

        fetch(block, 0).wait()
        tile(0, True)

        def one_slot(slot, inner):
            fetch(block, slot).wait()
            tile(slot, False)
            return inner

        lax.fori_loop(1, live(block), one_slot, 0)
        for part in range(BLK // ROWS):
            rows = pl.ds(part * ROWS, ROWS)
            o_ref[pl.ds(pl.multiple_of(base + part * ROWS, ROWS), ROWS), :] = (
                acc_ref[rows, :HD] / acc_ref[rows, HD:]
            ).astype(jnp.bfloat16)
        return carry

    lax.fori_loop(0, blocks, one_block, 0)


def attention(lists, query, kv_all):
    return pl.pallas_call(
        attention_kernel,
        out_shape=jax.ShapeDtypeStruct(query.shape, jnp.bfloat16),
        in_specs=[
            pl.BlockSpec(memory_space=pltpu.SMEM),
            pl.BlockSpec(memory_space=pltpu.VMEM),
            pl.BlockSpec(memory_space=pl.ANY),
        ],
        out_specs=pl.BlockSpec(memory_space=pltpu.VMEM),
        scratch_shapes=[
            pltpu.VMEM((2, KSEL, BLK, 2 * HD), jnp.bfloat16),
            pltpu.VMEM((BLK, HD), jnp.float32),
            pltpu.VMEM((BLK, 2 * HD), jnp.float32),
            pltpu.SemaphoreType.DMA((2, KSEL)),
        ],
        compiler_params=pltpu.CompilerParams(vmem_limit_bytes=48 << 20),
        name="block_attention",
    )(lists, query, kv_all)


def local(hidden_in, norm_gain, w_qkv, w_out, block_lists):
    section_id = lax.axis_index("section")
    width = w_qkv.shape[2]
    blocks_here = block_lists.shape[0]
    tok_dev = blocks_here * BLK
    resid = hidden_in.astype(jnp.float32)
    normed = (
        resid * lax.rsqrt(jnp.mean(resid * resid, axis=-1, keepdims=True) + EPS) * norm_gain
    ).astype(jnp.bfloat16)
    flat_weight = w_qkv.reshape(D, 3 * width)
    frequency = THETA ** (-(2.0 * jnp.arange(HD // 2, dtype=jnp.float32)) / HD)
    piece = lax.all_gather(normed, "head", axis=0, tiled=True)
    count = piece.shape[0]
    rows = jnp.dot(piece, flat_weight, preferred_element_type=jnp.float32)
    positions = (section_id * tok_dev + jnp.arange(count, dtype=jnp.int32)).astype(jnp.float32)
    angle = positions[:, None] * frequency[None, :]
    cosine = jnp.cos(angle)
    sine = jnp.sin(angle)
    query = (rotate(rows[:, :HD], cosine, sine) * QSCALE).astype(jnp.bfloat16)
    key_value = jnp.concatenate(
        [rotate(rows[:, HD : 2 * HD], cosine, sine), rows[:, 2 * HD :]], axis=1
    ).astype(jnp.bfloat16)
    kv_all = lax.all_gather(key_value, "section", axis=0, tiled=True)
    attended = attention(block_lists, query, kv_all)
    regrouped = lax.all_to_all(attended, "head", split_axis=0, concat_axis=1, tiled=True)
    summed = jnp.dot(
        regrouped,
        lax.all_gather(w_out, "head", axis=0, tiled=True),
        preferred_element_type=jnp.float32,
    )
    return (resid + summed).astype(jnp.bfloat16)


def solution(mesh):
    placed = (
        P(("section", "head"), None),
        P(),
        P(None, None, "head"),
        P("head", None),
        P("section", None),
    )
    return jax.shard_map(
        local, mesh=mesh, in_specs=placed, out_specs=P(("section", "head"), None), check_vma=False
    )
```

time: 566 us -> 288 us (0.51)
  matrix products: 181 us -> 15.3 us
  loops' own time: 92.6 us -> 0 us
  local copies, waits for them, and re-layouts: 66.8 us -> 0.8 us
  Pallas kernels: 0 us -> 63.2 us
  other arithmetic: 36.6 us -> 15.6 us
  waiting for transfers between devices: 165 us -> 173 us
    dot_general x133 -> x1, matrix products: 175 us -> 9.25 us  [local(): rows = jnp.dot(piece, flat_weight, preferred_element_type=jnp.float32)]
    another operation x7 -> x0, loops' own time: 92.6 us -> none  [the longest x6 88.2 us: one_block(): lax.fori_loop(0, live_slots, one_slot, start_state)]
    pallas_call x0 -> x1, Pallas kernels: none -> 63.2 us  [attention(): pl.pallas_call(attention_kernel, out_shape=jax.ShapeDtypeStruct(query.sha...]
    dynamic_slice x72 -> x0, local copies, waits for them, and re-layouts: 40.5 us -> none  [the longest x66 36.5 us: one_slot(): source = block_row[slot]]
    reduce_sum x72 -> x0, other arithmetic: 21.3 us -> none  [the longest x66 13 us: one_slot(): total = total * factor + jnp.sum(weights, axis=-1)]
    while x69 -> x0, local copies, waits for them, and re-layouts: 18.2 us -> none  [the longest x3 18 us: local(): lax.scan(one_block, jnp.zeros((), jnp.int32), (query_blocks, block_lists,...]
    all_gather x1, waiting for transfers between devices: 0.02 us -> 16.3 us  [local(): lax.all_gather(w_out, 'head', axis=0, tiled=True)]
    another operation x0 -> x1, other arithmetic: none -> 8.09 us
  transfers between devices with their start and end apart: 5 -> 4, of which waited for: 4 -> 4; matrix products, arithmetic and copies ran while one was open for 47% -> 1% of each run, Pallas kernels for 0% -> 22%
where the time goes in v1:
time: 288 us
  waiting for transfers between devices  173 us (60%)
  Pallas kernels  63.2 us (22%)
  other arithmetic  15.6 us (5%)
  matrix products  15.3 us (5%)
  between operations  13.2 us (5%)
  starting transfers between devices  6.93 us (2%)
    all_gather x1, waiting for transfers between devices, local(): piece = lax.all_gather(normed, 'head', axis=0, tiled=True)  90.1 us
    pallas_call x1, Pallas kernels, attention(): pl.pallas_call(attention_kernel, out_shape=jax.ShapeDtypeStruct(query.sha...  63.2 us
    all_gather x1, waiting for transfers between devices, local(): kv_all = lax.all_gather(key_value, 'section', axis=0, tiled=True)  63.1 us
    all_gather x1, waiting for transfers between devices, local(): lax.all_gather(w_out, 'head', axis=0, tiled=True)  16.3 us
    dot_general x1, matrix products, local(): rows = jnp.dot(piece, flat_weight, preferred_element_type=jnp.float32)  9.25 us
    another operation x1, other arithmetic  8.09 us
    all_to_all x1, starting transfers between devices, local(): lax.all_to_all(attended, 'head', split_axis=0, concat_axis=1, tiled=True)  6.85 us
    dot_general x1, matrix products, local(): jnp.dot(regrouped, lax.all_gather(w_out, 'head', axis=0, tiled=True), pre...  6.06 us
  transfers between devices with their start and end apart: 4, of which 4 were waited for; matrix products, arithmetic and copies ran while one was open for 1% of the time, Pallas kernels for 22%

profile of v1, /device:TPU:97, one launch (start us, length us, event | category | flops | bytes accessed | tf_op | source)
XLA Modules:
  0.0 287.9 jit_solution(6842036084635680766)
XLA Ops:
  6.5 0.0 all-gather.4.cloned.1.call-start
  6.5 1.5 fusion.15
  8.0 2.3 fusion.17
  10.3 0.0 all-gather.4.cloned.1.call-update
  10.3 0.0 all-gather.6.cloned.1.call-start
  10.4 0.7 copy.18
  11.1 90.1 %all-gather.4.cloned.1.call-done = bf16[3072,2048]{1,0:T(8,128)(2,1)} async-done(((bf16[192,2048]{1,0:T(8,128)(2,1)}), bf16[3072,2048]{1,0:T(8,128)(2,1)}) %all-gather.4.cloned.1.call-update) | async-done | bytes 12582928 | tf_op jit(solution)/shard_map/all_gather | solution.py:143
  101.3 9.2 %fusion.21 = f32[3072,384]{1,0:T(8,128)S(1)} fusion(bf16[3072,2048]{1,0:T(8,128)(2,1)} %all-gather.4.cloned.1.call-done, bf16[2048,384]{0,1:T(8,128)(2,1)S(1)} %bitcast.13), kind=kOutput, calls=%fused_computation.32 | convolution fusion | flops 4831838208 | bytes 18874368 | tf_op jit(solution)/shard_map/dot_general | solution.py:145
  110.5 0.1 slice.41
  110.6 8.1 %fusion.12 = (bf16[3072,64]{1,0:T(8,128)(2,1)S(1)}, bf16[3072,64]{1,0:T(8,128)(2,1)S(1)}, f32[3072,64]{1,0:T(8,128)S(1)}, f32[3072,64]{1,0:T(8,128)}) fusion(f32[3072,384]{1,0:T(8,128)S(1)} %fusion.21, f32[64]{0:T(128)S(1)} %multiply_power_fusion, f32[3072]{0:T(1024)S(1)} %add_convert_fusion), kind=kLoop, calls=%fused_computation.17 | loop fusion | flops 2949120 | bytes 5517568 | tf_op jit(solution)/shard_map/convert
  118.7 1.9 pad_maximum_fusion
  120.6 0.0 all-gather.6.cloned.1.call-update
  120.6 0.0 all-gather.8.cloned.1.call-start
  120.6 0.7 all-gather.8.cloned.1.call-update
  121.3 0.0 copy-start
  121.3 1.9 fusion.18.q_ref
  123.2 63.1 %all-gather.6.cloned.1.call-done.kv_hbm = bf16[24576,256]{1,0:T(8,128)(2,1)} async-done(((bf16[3072,256]{1,0:T(8,128)(2,1)}), bf16[24576,256]{1,0:T(8,128)(2,1)}) %all-gather.6.cloned.1.call-update) | async-done | bytes 12582928 | tf_op jit(solution)/shard_map/all_gather | solution.py:154
  186.3 0.0 copy-done
  186.3 63.2 %block_attention.1 = bf16[3072,128]{1,0:T(8,128)(2,1)} custom-call(s32[6,12]{1,0:T(8,128)S(1)} %copy-done, bf16[3072,128]{1,0:T(8,128)(2,1)S(1)} %fusion.18.q_ref, bf16[24576,256]{1,0:T(8,128)(2,1)} %all-gather.6.cloned.1.call-done.kv_hbm), custom_call_target="tpu_custom_call" | custom-call | tf_op jit(solution)/shard_map/block_attention/pallas_call | solution.py:112
  249.6 0.0 copy-start.1
  249.6 6.8 %all-to-all-start = ((bf16[16,192,128]{2,1,0:T(8,128)(2,1)}), bf16[16,192,128]{2,1,0:T(8,128)(2,1)S(1)}, u32[]{:S(2)}, u32[]{:S(2)}) async-start(bf16[16,192,128]{2,1,0:T(8,128)(2,1)} %bitcast.1), calls=%async_computation | async-start | bytes 1572864 | tf_op jit(solution)/shard_map/all_to_all | solution.py:156
  256.4 16.3 %all-gather.8.cloned.1.call-done = bf16[2048,2048]{1,0:T(8,128)(2,1)} async-done(((bf16[128,2048]{1,0:T(8,128)(2,1)}), bf16[2048,2048]{1,0:T(8,128)(2,1)}) %all-gather.8.cloned.1.call-update) | async-done | bytes 8388624 | tf_op jit(solution)/shard_map/all_gather | solution.py:159
  272.7 2.6 all-to-all-done
  275.3 6.1 %fusion = bf16[192,2048]{1,0:T(8,128)(2,1)} fusion(bf16[2048,2048]{1,0:T(8,128)(2,1)} %all-gather.8.cloned.1.call-done, bf16[192,2048]{1,0:T(8,128)(2,1)S(1)} %copy-done.1, bf16[16,192,128]{2,1,0:T(8,128)(2,1)S(1)} %all-to-all-done), kind=kOutput, calls=%fused_computation.1 | convolution fusion | flops 1611792384 | bytes 10747904 | tf_op jit(solution)/shard_map/dot_general | solution.py:157
  (6 shorter events, 0.0 us)
Async XLA Ops:
  6.5 3.8 %copy-start.2 = (bf16[2048,3,128]{2,0,1:T(8,128)(2,1)S(1)}, bf16[2048,3,128]{2,0,1:T(8,128)(2,1)}, u32[]{:S(2)}) copy-start(bf16[2048,3,128]{2,0,1:T(8,128)(2,1)} %param.7) | copy-start | bytes 4718596
  6.5 94.7 %all-gather.4.cloned.1.call-start = ((), (), s32[]{:S(2)}) async-start(), calls=%async_computation.1 | async-start | bytes 13369344 | tf_op jit(solution)/shard_map/all_gather | solution.py:143
  10.3 176.0 %all-gather.6.cloned.1.call-start = ((), (), s32[]{:S(2)}) async-start(), calls=%async_computation.2 | async-start | bytes 14155776 | tf_op jit(solution)/shard_map/all_gather | solution.py:154
  120.6 152.1 %all-gather.8.cloned.1.call-start = ((), (), s32[]{:S(2)}) async-start(), calls=%async_computation.3 | async-start | bytes 8912896 | tf_op jit(solution)/shard_map/all_gather | solution.py:159
  121.3 65.0 %copy-start = (s32[6,12]{1,0:T(8,128)S(1)}, s32[6,12]{1,0:T(8,128)}, u32[]{:S(2)}) copy-start(s32[6,12]{1,0:T(8,128)} %lists.1) | copy-start | bytes 868
  249.6 25.7 %copy-start.1 = (bf16[192,2048]{1,0:T(8,128)(2,1)S(1)}, bf16[192,2048]{1,0:T(8,128)(2,1)}, u32[]{:S(2)}) copy-start(bf16[192,2048]{1,0:T(8,128)(2,1)} %param.5) | copy-start | bytes 2359300
  249.6 25.7 %all-to-all-start = ((bf16[16,192,128]{2,1,0:T(8,128)(2,1)}), bf16[16,192,128]{2,1,0:T(8,128)(2,1)S(1)}, u32[]{:S(2)}, u32[]{:S(2)}) async-start(bf16[16,192,128]{2,1,0:T(8,128)(2,1)} %bitcast.1), calls=%async_computation | async-start | bytes 1572864 | tf_op jit(solution)/shard_map/all_to_all | solution.py:156
Sparse Core Ops, SparseCore 0:
  10.4 90.7 all-gather.3
  120.7 65.5 all-gather.5
  188.5 84.1 all-gather.7

commit v2 on v1

v2 whole, which is shorter than its diff:
```python
import math

import jax
import jax.numpy as jnp
from jax import lax
from jax.experimental import pallas as pl
from jax.experimental.pallas import tpu as pltpu
from jax.sharding import PartitionSpec as P

D = 2048
HD = 128
BLK = 512
KSEL = 12
NBLK = 48
SECTIONS = 8
HEADS = 16

EPS = 1e-05
THETA = 10000.0
QSCALE = math.log2(math.e) / math.sqrt(HD)
ROWS = 256

PIECE = 192
HALF = PIECE // 2
UNIT = HALF // 2
TOK = PIECE * HEADS
LAST = HEADS // 2
MESH = pl.DeviceIdType.MESH


def layer_kernel(
    lists, xn, w_ref, cos_b, sin_b, cos_r, sin_r, o_ref,
    x_all, kv_all, q_ref, m_ref, acc_ref,
    ring_send, ring_recv, z_send, z_recv, s_send, s_recv,
):
    section = lax.axis_index("section")
    head = lax.axis_index("head")
    ypos, xpos = head // 4, head % 4
    diagonal = (xpos + ypos) % 4
    spot = (4 * ypos + diagonal, 4 * xpos + diagonal)

    def head_of(ring, place):
        place = (place + 2 * HEADS) % HEADS
        slow, fast = place // 4, place % 4
        other = (fast - slow + 4) % 4
        return slow * 4 + other if ring == 0 else other * 4 + slow

    def ring_device(ring, way):
        return {"section": section, "head": head_of(ring, spot[ring] + (1 if way == 0 else -1))}

    ring_to = [[ring_device(ring, way) for way in range(2)] for ring in range(2)]
    z_up = {"section": (section + 2) % SECTIONS, "head": head}
    z_down = {"section": (section + SECTIONS - 2) % SECTIONS, "head": head}
    partner = {"section": section + 1 - 2 * (section % 2), "head": head}

    barrier = pltpu.get_barrier_semaphore()
    for device in (*ring_to[0], *ring_to[1], z_up, z_down, partner):
        pl.semaphore_signal(barrier, inc=1, device_id=device, device_id_type=MESH)
    pl.semaphore_wait(barrier, 7)

    def rows_of(start, size):
        return pl.ds(pl.multiple_of(start, 16), size)

    def send(source, target, send_sem, recv_sem, device):
        pltpu.make_async_remote_copy(
            src_ref=source,
            dst_ref=target,
            send_sem=send_sem,
            recv_sem=recv_sem,
            device_id=device,
            device_id_type=MESH,
        ).start()

    def arrived(ref, rows, sem):
        view = ref.at[pl.ds(0, rows), :]
        pltpu.make_async_copy(view, view, sem).wait()

    def origin(ring, way, step):
        return head_of(ring, spot[ring] + (step if way == 1 else -step))

    def unit_rows(ring, source, unit):
        return rows_of(source * PIECE + ring * HALF + unit * UNIT, UNIT)

    def pass_on(ring, way, unit, step, source):
        rows = unit_rows(ring, source, unit)
        send(
            x_all.at[rows, :],
            x_all.at[rows, :],
            ring_send,
            ring_recv.at[ring, way, unit, step + 1],
            ring_to[ring][way],
        )

    def starts_of(step):
        if isinstance(step, int) and step == 0:
            return [(head, 0), (head, 1)]
        if isinstance(step, int) and step == LAST:
            return [(origin(ring, 0, LAST), ring) for ring in range(2)]
        return [(origin(ring, way, step), ring) for ring in range(2) for way in range(2)]

    def project(tokens, pieces):
        result = jnp.dot(tokens, w_ref[...], preferred_element_type=jnp.float32)
        for index, (source, ring) in enumerate(pieces):
            part = result[index * HALF : (index + 1) * HALF]
            base_cos, base_sin = cos_b[pl.ds(source, 1), :], sin_b[pl.ds(source, 1), :]
            row_cos = cos_r[ring * HALF : (ring + 1) * HALF, :]
            row_sin = sin_r[ring * HALF : (ring + 1) * HALF, :]
            cosine = base_cos * row_cos - base_sin * row_sin
            sine = base_sin * row_cos + base_cos * row_sin
            query, key, value = part[:, :HD], part[:, HD : 2 * HD], part[:, 2 * HD :]
            query = (query * cosine + pltpu.roll(query, HD // 2, 1) * sine) * QSCALE
            key = key * cosine + pltpu.roll(key, HD // 2, 1) * sine
            start = source * PIECE + ring * HALF
            q_ref[rows_of(start, HALF), :] = query.astype(jnp.bfloat16)
            own = rows_of(section * TOK + start, HALF)
            kv_all[own, :HD] = key.astype(jnp.bfloat16)
            kv_all[own, HD:] = value.astype(jnp.bfloat16)

    def kv_copy(region, start, size, send_sem, recv_sem, device):
        rows = rows_of(region * TOK + start, size)
        send(kv_all.at[rows, :], kv_all.at[rows, :], send_sem, recv_sem, device)

    def share(step, pieces):
        for source, ring in pieces:
            start = source * PIECE + ring * HALF
            kv_copy(section, start, HALF, z_send, z_recv.at[0, step], z_up)
            kv_copy(section, start, HALF, z_send, z_recv.at[1, step], z_down)
            kv_copy(section, start, HALF, s_send, s_recv.at[step], partner)

    def relay_near(step, pieces):
        below, above = (section + SECTIONS - 2) % SECTIONS, (section + 2) % SECTIONS
        arrived(kv_all, len(pieces) * HALF, z_recv.at[0, step])
        for source, ring in pieces:
            start = source * PIECE + ring * HALF
            kv_copy(below, start, UNIT, z_send, z_recv.at[2, step], z_up)
            kv_copy(below, start, HALF, s_send, s_recv.at[step], partner)
        arrived(kv_all, len(pieces) * HALF, z_recv.at[1, step])
        for source, ring in pieces:
            start = source * PIECE + ring * HALF
            kv_copy(above, start + UNIT, UNIT, z_send, z_recv.at[3, step], z_down)
            kv_copy(above, start, HALF, s_send, s_recv.at[step], partner)

    def relay_far(step, pieces):
        across = (section + 4) % SECTIONS
        arrived(kv_all, len(pieces) * UNIT, z_recv.at[2, step])
        arrived(kv_all, len(pieces) * UNIT, z_recv.at[3, step])
        for source, ring in pieces:
            start = source * PIECE + ring * HALF
            kv_copy(across, start, HALF, s_send, s_recv.at[step], partner)

    for unit in range(2):
        for ring in range(2):
            for way in range(2):
                send(
                    xn.at[pl.ds(ring * HALF + unit * UNIT, UNIT), :],
                    x_all.at[unit_rows(ring, head, unit), :],
                    ring_send,
                    ring_recv.at[ring, way, unit, 1],
                    ring_to[ring][way],
                )
    project(xn[...], starts_of(0))
    share(0, starts_of(0))
    relay_near(0, starts_of(0))

    def one_step(step, carry):
        for unit in range(2):
            for ring in range(2):
                for way in range(2):
                    arrived(x_all, UNIT, ring_recv.at[ring, way, unit, step])
                    source = origin(ring, way, step)
                    if way == unit:
                        pass_on(ring, way, unit, step, source)
                    else:

                        @pl.when(step < LAST - 1)
                        def _(ring=ring, way=way, unit=unit, source=source):
                            pass_on(ring, way, unit, step, source)

        pieces = starts_of(step)
        tokens = jnp.concatenate(
            [x_all[rows_of(source * PIECE + ring * HALF, HALF), :] for source, ring in pieces],
            axis=0,
        )
        project(tokens, pieces)

        @pl.when(step >= 2)
        def _():
            relay_near(step - 1, starts_of(step - 1))

        @pl.when(step >= 3)
        def _():
            relay_far(step - 2, starts_of(step - 2))

        share(step, pieces)
        return carry

    lax.fori_loop(1, LAST, one_step, 0)
    relay_far(0, starts_of(0))
    for ring in range(2):
        for way in range(2):
            arrived(x_all, UNIT, ring_recv.at[ring, way, way, LAST])
    pieces = starts_of(LAST)
    tokens = jnp.concatenate(
        [x_all[rows_of(source * PIECE + ring * HALF, HALF), :] for source, ring in pieces], axis=0
    )
    project(tokens, pieces)
    relay_near(LAST - 1, starts_of(LAST - 1))
    relay_far(LAST - 2, starts_of(LAST - 2))
    share(LAST, pieces)
    relay_far(LAST - 1, starts_of(LAST - 1))
    relay_near(LAST, pieces)
    relay_far(LAST, pieces)
    for step in range(LAST + 1):
        arrived(kv_all, 4 * HALF * (2 if step in (0, LAST) else 4), s_recv.at[step])

    blocks = TOK // BLK
    ones = jnp.ones((BLK, HD), jnp.bfloat16)

    def one_block(block, carry):
        base = pl.multiple_of(block * BLK, BLK)
        count = 1 + ((section * blocks + block) * (KSEL - 1)) // (NBLK - 1)

        def tile(source, first):
            keys = kv_all[pl.ds(source * BLK, BLK), :HD]
            values = jnp.concatenate([kv_all[pl.ds(source * BLK, BLK), HD:], ones], axis=1)
            for part in range(BLK // ROWS):
                rows = pl.ds(part * ROWS, ROWS)
                query = q_ref[pl.ds(pl.multiple_of(base + part * ROWS, ROWS), ROWS), :]
                scores = lax.dot_general(
                    query, keys, (((1,), (1,)), ((), ())), preferred_element_type=jnp.float32
                )
                if first:
                    row = lax.broadcasted_iota(jnp.int32, (ROWS, BLK), 0) + part * ROWS
                    col = lax.broadcasted_iota(jnp.int32, (ROWS, BLK), 1)
                    scores = jnp.where(col <= row, scores, -jnp.inf)
                peak = jnp.max(scores, axis=1, keepdims=True)
                if not first:
                    old = m_ref[rows, :1]
                    peak = jnp.maximum(peak, old)
                weights = jnp.exp2(scores - peak).astype(jnp.bfloat16)
                update = jnp.dot(weights, values, preferred_element_type=jnp.float32)
                if first:
                    acc_ref[rows, :] = update
                else:
                    acc_ref[rows, :] = acc_ref[rows, :] * jnp.exp2(old - peak) + update
                m_ref[rows, :] = jnp.broadcast_to(peak, (ROWS, HD))

        tile(section * blocks + block, True)

        def one_slot(slot, inner):
            tile(lists[block, slot], False)
            return inner

        lax.fori_loop(1, count, one_slot, 0)
        for part in range(BLK // ROWS):
            rows = pl.ds(part * ROWS, ROWS)
            o_ref[pl.ds(pl.multiple_of(base + part * ROWS, ROWS), ROWS), :] = (
                acc_ref[rows, :HD] / acc_ref[rows, HD:]
            ).astype(jnp.bfloat16)
        return carry

    lax.fori_loop(0, blocks, one_block, 0)

    arrived(x_all, 4 * (2 * LAST - 1) * UNIT, ring_send)
    arrived(kv_all, 3 * TOK, z_send)
    arrived(kv_all, 4 * TOK, s_send)


def attend(lists, normed, weight, tables):
    vmem = pl.BlockSpec(memory_space=pltpu.VMEM)
    return pl.pallas_call(
        layer_kernel,
        out_shape=jax.ShapeDtypeStruct((TOK, HD), jnp.bfloat16),
        in_specs=[pl.BlockSpec(memory_space=pltpu.SMEM)] + [vmem] * 6,
        out_specs=vmem,
        scratch_shapes=[
            pltpu.VMEM((TOK, D), jnp.bfloat16),
            pltpu.VMEM((SECTIONS * TOK, 2 * HD), jnp.bfloat16),
            pltpu.VMEM((TOK, HD), jnp.bfloat16),
            pltpu.VMEM((BLK, HD), jnp.float32),
            pltpu.VMEM((BLK, 2 * HD), jnp.float32),
            pltpu.SemaphoreType.DMA,
            pltpu.SemaphoreType.DMA((2, 2, 2, LAST + 1)),
            pltpu.SemaphoreType.DMA,
            pltpu.SemaphoreType.DMA((4, LAST + 1)),
            pltpu.SemaphoreType.DMA,
            pltpu.SemaphoreType.DMA((LAST + 1,)),
        ],
        compiler_params=pltpu.CompilerParams(
            collective_id=0, has_side_effects=True, vmem_limit_bytes=56 << 20
        ),
        name="layer",
    )(lists, normed, weight, *tables)


def rotary_tables(positions):
    frequency = THETA ** (-(2.0 * jnp.arange(HD // 2, dtype=jnp.float32)) / HD)
    angle = positions.astype(jnp.float32)[:, None] * frequency[None, :]
    cosine, sine = jnp.cos(angle), jnp.sin(angle)
    return jnp.concatenate([cosine, cosine], axis=1), jnp.concatenate([-sine, sine], axis=1)


def local(hidden_in, norm_gain, w_qkv, w_out, block_lists):
    section_id = lax.axis_index("section")
    resid = hidden_in.astype(jnp.float32)
    normed = (
        resid * lax.rsqrt(jnp.mean(resid * resid, axis=-1, keepdims=True) + EPS) * norm_gain
    ).astype(jnp.bfloat16)
    flat_weight = w_qkv.reshape(D, 3 * HD)
    bases = section_id * TOK + PIECE * jnp.arange(HEADS, dtype=jnp.int32)
    cos_b, sin_b = rotary_tables(bases)
    cos_r, sin_r = rotary_tables(jnp.arange(PIECE, dtype=jnp.int32))
    attended = attend(block_lists, normed, flat_weight, (cos_b, sin_b, cos_r, sin_r))
    regrouped = lax.all_to_all(attended, "head", split_axis=0, concat_axis=1, tiled=True)
    summed = jnp.dot(
        regrouped,
        lax.all_gather(w_out, "head", axis=0, tiled=True),
        preferred_element_type=jnp.float32,
    )
    return (resid + summed).astype(jnp.bfloat16)


def solution(mesh):
    placed = (
        P(("section", "head"), None),
        P(),
        P(None, None, "head"),
        P("head", None),
        P("section", None),
    )
    return jax.shard_map(
        local, mesh=mesh, in_specs=placed, out_specs=P(("section", "head"), None), check_vma=False
    )
```

time: 288 us -> 233 us (0.81)
  waiting for transfers between devices: 173 us -> 0.71 us
  Pallas kernels: 63.2 us -> 191 us
  blocking collectives: 0 us -> 14.4 us
  other arithmetic: 15.6 us -> 3.42 us
  matrix products: 15.3 us -> 6.06 us
  starting transfers between devices: 6.93 us -> 0.01 us
    all_gather x2 -> x0, waiting for transfers between devices: 153 us -> none  [the longest x1 90.1 us: local(): piece = lax.all_gather(normed, 'head', axis=0, tiled=True)]
    pallas_call x1, Pallas kernels: 63.2 us -> 191 us  [attend(): pl.pallas_call(layer_kernel, out_shape=jax.ShapeDtypeStruct((TOK, HD), jn...]
    all_gather x1, waiting for transfers between devices: 16.3 us -> 0.01 us  [local(): lax.all_gather(w_out, 'head', axis=0, tiled=True)]
    all_to_all x0 -> x1, blocking collectives: none -> 14.4 us  [local(): lax.all_to_all(attended, 'head', split_axis=0, concat_axis=1, tiled=True)]
    dot_general x1 -> x0, matrix products: 9.25 us -> none  [local(): rows = jnp.dot(piece, flat_weight, preferred_element_type=jnp.float32)]
    another operation x1 -> x0, other arithmetic: 8.09 us -> none
    all_to_all x1 -> x0, starting transfers between devices: 6.85 us -> none  [local(): lax.all_to_all(attended, 'head', split_axis=0, concat_axis=1, tiled=True)]
  transfers between devices with their start and end apart: 4 -> 1, of which waited for: 4 -> 0; matrix products, arithmetic and copies ran while one was open for 1% -> 3% of each run, Pallas kernels for 22% -> 82%
where the time goes in v2:
time: 233 us; the launch traced here: 232 us
  Pallas kernels  191 us (82%)
  blocking collectives  14.4 us (6%)
  between operations  13.4 us (6%)
  matrix products  6.06 us (3%)
  other arithmetic  3.42 us (1%)
  local copies, waits for them, and re-layouts  3.36 us (1%)
    pallas_call x1, Pallas kernels, attend(): pl.pallas_call(layer_kernel, out_shape=jax.ShapeDtypeStruct((TOK, HD), jn...  191 us
    all_to_all x1, blocking collectives, local(): lax.all_to_all(attended, 'head', split_axis=0, concat_axis=1, tiled=True)  14.4 us
    dot_general x1, matrix products, local(): jnp.dot(regrouped, lax.all_gather(w_out, 'head', axis=0, tiled=True), pre...  6.06 us
  transfers between devices with their start and end apart: 1, of which 0 were waited for; matrix products, arithmetic and copies ran while one was open for 3% of the time, Pallas kernels for 82%

profile of v2, /device:TPU:97, one launch (start us, length us, event | category | flops | bytes accessed | tf_op | source)
XLA Modules:
  0.0 232.3 jit_solution(16138961763468692192)
XLA Ops:
  6.5 0.0 all-gather.2.cloned.1.call-start
  6.5 0.7 all-gather.2.cloned.1.call-update
  7.3 1.7 copy.10
  9.0 0.0 copy-start
  9.0 1.6 copy.11.w_ref
  10.6 0.0 copy-start.1
  10.7 0.1 fusion.7
  10.8 0.7 pad_maximum_fusion.2
  11.5 0.4 fusion.6
  11.9 0.8 pad_maximum_fusion
  12.7 0.0 copy-done
  12.7 0.2 fusion.1
  13.0 0.0 copy-done.1
  13.0 1.1 fusion.3.xn
  14.1 190.9 %layer.1 = bf16[3072,128]{1,0:T(8,128)(2,1)} custom-call(s32[6,12]{1,0:T(8,128)} %lists.1, bf16[192,2048]{1,0:T(8,128)(2,1)} %fusion.3.xn, bf16[2048,384]{1,0:T(8,128)(2,1)} %copy.11.w_ref, f32[16,128]{1,0:T(8,128)} %get-tuple-element.11.cos_b, f32[16,128]{1,0:T(8,128)} %get-tuple-element.12.sin_b, f32[192,128]{1,0:T(8,128)} %get-tuple-element.13.cos_r, ...), custom_call_target="tpu_custom_call" | custom-call | tf_op jit(solution)/shard_map/layer/pallas_call | solution.py:271
  205.0 14.4 %all_to_all.19 = bf16[16,192,128]{2,1,0:T(8,128)(2,1)S(1)} all-to-all(bf16[16,192,128]{2,1,0:T(8,128)(2,1)} %bitcast.12), channel_id=1, replica_groups=mesh['section'=8,'head'=16] {'head'}, dimensions={0} | all-to-all | bytes 1572864 | tf_op jit(solution)/shard_map/all_to_all | solution.py:314
  219.4 0.0 all-gather.2.cloned.1.call-done
  219.4 6.1 %fusion = bf16[192,2048]{1,0:T(8,128)(2,1)} fusion(bf16[2048,2048]{1,0:T(8,128)(2,1)} %all-gather.2.cloned.1.call-done, bf16[192,2048]{1,0:T(8,128)(2,1)S(1)} %copy-done, bf16[16,192,128]{2,1,0:T(8,128)(2,1)S(1)} %all_to_all.19), kind=kOutput, calls=%fused_computation.1 | convolution fusion | flops 1611792384 | bytes 10747904 | tf_op jit(solution)/shard_map/dot_general | solution.py:315
  (4 shorter events, 0.0 us)
Async XLA Ops:
  6.5 212.8 %all-gather.2.cloned.1.call-start = ((), (), s32[]{:S(2)}) async-start(), calls=%async_computation.1 | async-start | bytes 8912896 | tf_op jit(solution)/shard_map/all_gather | solution.py:317
  9.0 3.7 %copy-start = (bf16[192,2048]{1,0:T(8,128)(2,1)S(1)}, bf16[192,2048]{1,0:T(8,128)(2,1)}, u32[]{:S(2)}) copy-start(bf16[192,2048]{1,0:T(8,128)(2,1)} %param.5) | copy-start | bytes 2359300
  10.6 2.3 %copy-start.1 = (f32[2048]{0:T(1024)S(1)}, f32[2048]{0:T(1024)}, u32[]{:S(2)}) copy-start(f32[2048]{0:T(1024)} %param.6) | copy-start | bytes 24580
Sparse Core Ops, SparseCore 0:
  9.5 111.8 all-gather.1

commit v3 on v2

--- a/solution.py
+++ b/solution.py
@@ -25,13 +25,18 @@
 UNIT = HALF // 2
 TOK = PIECE * HEADS
 LAST = HEADS // 2
+W_HALF = HD // 2
+W_PART = W_HALF // 2
+W_BLOCK = 3
+OUT_TILE = 256
 MESH = pl.DeviceIdType.MESH
 
 
 def layer_kernel(
-    lists, xn, w_ref, cos_b, sin_b, cos_r, sin_r, o_ref,
-    x_all, kv_all, q_ref, m_ref, acc_ref,
+    lists, hidden, xn, w_ref, shard, cos_b, sin_b, cos_r, sin_r, out_ref,
+    x_all, kv_all, q_ref, m_ref, acc_ref, o_ref, w_all, mix,
     ring_send, ring_recv, z_send, z_recv, s_send, s_recv,
+    w_send, w_recv, wp_send, wp_recv, w_own, a_send, a_recv, a_own,
 ):
     section = lax.axis_index("section")
     head = lax.axis_index("head")
@@ -54,9 +59,16 @@
     partner = {"section": section + 1 - 2 * (section % 2), "head": head}
 
     barrier = pltpu.get_barrier_semaphore()
-    for device in (*ring_to[0], *ring_to[1], z_up, z_down, partner):
+    for device in (z_up, z_down, partner):
         pl.semaphore_signal(barrier, inc=1, device_id=device, device_id_type=MESH)
-    pl.semaphore_wait(barrier, 7)
+
+    def greet(step, carry):
+        peer = {"section": section, "head": (head + step) % HEADS}
+        pl.semaphore_signal(barrier, inc=1, device_id=peer, device_id_type=MESH)
+        return carry
+
+    lax.fori_loop(1, HEADS, greet, 0)
+    pl.semaphore_wait(barrier, HEADS + 2)
 
     def rows_of(start, size):
         return pl.ds(pl.multiple_of(start, 16), size)
@@ -99,7 +111,8 @@
         return [(origin(ring, way, step), ring) for ring in range(2) for way in range(2)]
 
     def project(tokens, pieces):
-        result = jnp.dot(tokens, w_ref[...], preferred_element_type=jnp.float32)
+        weight = jnp.concatenate([w_ref[0], w_ref[1], w_ref[2]], axis=1)
+        result = jnp.dot(tokens, weight, preferred_element_type=jnp.float32)
         for index, (source, ring) in enumerate(pieces):
             part = result[index * HALF : (index + 1) * HALF]
             base_cos, base_sin = cos_b[pl.ds(source, 1), :], sin_b[pl.ds(source, 1), :]
@@ -204,6 +217,37 @@
         [x_all[rows_of(source * PIECE + ring * HALF, HALF), :] for source, ring in pieces], axis=0
     )
     project(tokens, pieces)
+
+    core = section % 2
+    own_rows = pltpu.make_async_copy(
+        shard, w_all.at[rows_of(head * HD, HD), :], w_own
+    )
+    own_rows.start()
+
+    def w_rows(source, part):
+        return rows_of(source * HD + core * W_HALF + part * W_PART, W_PART)
+
+    def line(part, step):
+        if part == 0:
+            return ypos * 4 + (xpos + step) % 4
+        return ((ypos + step) % 4) * 4 + xpos
+
+    def w_copy(source, part, stage, target, own):
+        if own:
+            view = shard.at[rows_of(core * W_HALF + part * W_PART, W_PART), :]
+        else:
+            view = w_all.at[w_rows(source, part), :]
+        send(
+            view,
+            w_all.at[w_rows(source, part), :],
+            w_send,
+            w_recv.at[part, stage],
+            {"section": section, "head": target},
+        )
+
+    for part in range(2):
+        for step in range(1, 4):
+            w_copy(head, part, 0, line(part, step), True)
     relay_near(LAST - 1, starts_of(LAST - 1))
     relay_far(LAST - 2, starts_of(LAST - 2))
     share(LAST, pieces)
@@ -212,6 +256,40 @@
     relay_far(LAST, pieces)
     for step in range(LAST + 1):
         arrived(kv_all, 4 * HALF * (2 if step in (0, LAST) else 4), s_recv.at[step])
+
+    for part in range(2):
+        arrived(w_all, 3 * W_PART, w_recv.at[part, 0])
+        for step in range(1, 4):
+            for other in range(4):
+                w_copy(line(part, other), part, 1, line(1 - part, step), other == 0)
+
+    def w_to_partner():
+        for part in range(2):
+            arrived(w_all, 12 * W_PART, w_recv.at[part, 1])
+
+        def one(step, carry):
+            rows = rows_of(((head + step) % HEADS) * HD + core * W_HALF, W_HALF)
+            send(w_all.at[rows, :], w_all.at[rows, :], wp_send, wp_recv, partner)
+            return carry
+
+        lax.fori_loop(1, HEADS, one, 0)
+
+    own_columns = pl.ds(pl.multiple_of(head * HD, HD), HD)
+
+    def deliver(target, carry):
+        rows = rows_of(target * PIECE, PIECE)
+
+        @pl.when(target != head)
+        def _():
+            send(
+                o_ref.at[rows, :],
+                mix.at[:, own_columns],
+                a_send,
+                a_recv,
+                {"section": section, "head": target},
+            )
+
+        return carry
 
     blocks = TOK // BLK
     ones = jnp.ones((BLK, HD), jnp.bfloat16)
@@ -257,21 +335,51 @@
             o_ref[pl.ds(pl.multiple_of(base + part * ROWS, ROWS), ROWS), :] = (
                 acc_ref[rows, :HD] / acc_ref[rows, HD:]
             ).astype(jnp.bfloat16)
+        lax.fori_loop((block * BLK) // PIECE, ((block + 1) * BLK) // PIECE, deliver, 0)
+
+        @pl.when(block == W_BLOCK)
+        def _():
+            w_to_partner()
+
         return carry
 
     lax.fori_loop(0, blocks, one_block, 0)
 
+    own_piece = pltpu.make_async_copy(
+        o_ref.at[rows_of(head * PIECE, PIECE), :], mix.at[:, own_columns], a_own
+    )
+    own_piece.start()
+    own_rows.wait()
+    arrived(w_all, (HEADS - 1) * W_HALF, wp_recv)
+    own_piece.wait()
+    taken = mix.at[:, pl.ds(0, (HEADS - 1) * HD)]
+    pltpu.make_async_copy(taken, taken, a_recv).wait()
+
+    def one_tile(tile, carry):
+        columns = pl.ds(pl.multiple_of(tile * OUT_TILE, OUT_TILE), OUT_TILE)
+        summed = jnp.dot(mix[...], w_all[:, columns], preferred_element_type=jnp.float32)
+        out_ref[:, columns] = (hidden[:, columns].astype(jnp.float32) + summed).astype(
+            jnp.bfloat16
+        )
+        return carry
+
+    lax.fori_loop(0, D // OUT_TILE, one_tile, 0)
+
+    arrived(w_all, 30 * W_PART, w_send)
+    arrived(w_all, (HEADS - 1) * W_HALF, wp_send)
+    pltpu.make_async_copy(taken, taken, a_send).wait()
     arrived(x_all, 4 * (2 * LAST - 1) * UNIT, ring_send)
     arrived(kv_all, 3 * TOK, z_send)
     arrived(kv_all, 4 * TOK, s_send)
 
 
-def attend(lists, normed, weight, tables):
+def layer(lists, hidden, normed, weight, shard, tables):
     vmem = pl.BlockSpec(memory_space=pltpu.VMEM)
+    dma = pltpu.SemaphoreType.DMA
     return pl.pallas_call(
         layer_kernel,
-        out_shape=jax.ShapeDtypeStruct((TOK, HD), jnp.bfloat16),
-        in_specs=[pl.BlockSpec(memory_space=pltpu.SMEM)] + [vmem] * 6,
+        out_shape=jax.ShapeDtypeStruct((PIECE, D), jnp.bfloat16),
+        in_specs=[pl.BlockSpec(memory_space=pltpu.SMEM)] + [vmem] * 8,
         out_specs=vmem,
         scratch_shapes=[
             pltpu.VMEM((TOK, D), jnp.bfloat16),
@@ -279,18 +387,29 @@
             pltpu.VMEM((TOK, HD), jnp.bfloat16),
             pltpu.VMEM((BLK, HD), jnp.float32),
             pltpu.VMEM((BLK, 2 * HD), jnp.float32),
-            pltpu.SemaphoreType.DMA,
-            pltpu.SemaphoreType.DMA((2, 2, 2, LAST + 1)),
-            pltpu.SemaphoreType.DMA,
-            pltpu.SemaphoreType.DMA((4, LAST + 1)),
-            pltpu.SemaphoreType.DMA,
-            pltpu.SemaphoreType.DMA((LAST + 1,)),
+            pltpu.VMEM((TOK, HD), jnp.bfloat16),
+            pltpu.VMEM((D, D), jnp.bfloat16),
+            pltpu.VMEM((PIECE, D), jnp.bfloat16),
+            dma,
+            dma((2, 2, 2, LAST + 1)),
+            dma,
+            dma((4, LAST + 1)),
+            dma,
+            dma((LAST + 1,)),
+            dma,
+            dma((2, 2)),
+            dma,
+            dma,
+            dma,
+            dma,
+            dma,
+            dma,
         ],
         compiler_params=pltpu.CompilerParams(
-            collective_id=0, has_side_effects=True, vmem_limit_bytes=56 << 20
+            collective_id=0, has_side_effects=True, vmem_limit_bytes=60 << 20
         ),
         name="layer",
-    )(lists, normed, weight, *tables)
+    )(lists, hidden, normed, weight, shard, *tables)
 
 
 def rotary_tables(positions):
@@ -306,18 +425,10 @@
     normed = (
         resid * lax.rsqrt(jnp.mean(resid * resid, axis=-1, keepdims=True) + EPS) * norm_gain
     ).astype(jnp.bfloat16)
-    flat_weight = w_qkv.reshape(D, 3 * HD)
+    weight = jnp.transpose(w_qkv, (1, 0, 2))
     bases = section_id * TOK + PIECE * jnp.arange(HEADS, dtype=jnp.int32)
-    cos_b, sin_b = rotary_tables(bases)
-    cos_r, sin_r = rotary_tables(jnp.arange(PIECE, dtype=jnp.int32))
-    attended = attend(block_lists, normed, flat_weight, (cos_b, sin_b, cos_r, sin_r))
-    regrouped = lax.all_to_all(attended, "head", split_axis=0, concat_axis=1, tiled=True)
-    summed = jnp.dot(
-        regrouped,
-        lax.all_gather(w_out, "head", axis=0, tiled=True),
-        preferred_element_type=jnp.float32,
-    )
-    return (resid + summed).astype(jnp.bfloat16)
+    tables = rotary_tables(bases) + rotary_tables(jnp.arange(PIECE, dtype=jnp.int32))
+    return layer(block_lists, hidden_in, normed, weight, w_out, tables)
 
 
 def solution(mesh):

time: 233 us -> 166 us (0.71)
  the two profiles are of different devices: /device:TPU:97 before, /device:TPU:123 now
where the time goes in v3:
time: 166 us
  Pallas kernels  159 us (96%)
  other arithmetic  4.62 us (3%)
  local copies, waits for them, and re-layouts  2.1 us (1%)
    pallas_call x1, Pallas kernels, layer(): pl.pallas_call(layer_kernel, out_shape=jax.ShapeDtypeStruct((PIECE, D), j...  159 us

profile of v3, /device:TPU:123, one launch (start us, length us, event | category | flops | bytes accessed | tf_op | source)
XLA Modules:
  0.0 165.7 jit_solution(5736674678452755153)
XLA Ops:
  0.0 0.0 copy-start
  0.0 0.0 copy-start.1
  0.0 1.4 fusion
  1.5 0.1 fusion.4
  1.6 0.7 pad_maximum_fusion.2
  2.3 0.4 fusion.3
  2.7 0.8 pad_maximum_fusion
  3.5 0.0 copy-done
  3.5 0.0 copy-done.1
  3.5 1.1 fusion.2.xn
  4.6 159.0 %layer.1 = bf16[192,2048]{1,0:T(8,128)(2,1)} custom-call(s32[6,12]{1,0:T(8,128)} %lists.1, bf16[192,2048]{1,0:T(8,128)(2,1)} %hidden.1, bf16[192,2048]{1,0:T(8,128)(2,1)} %fusion.2.xn, bf16[3,2048,128]{2,1,0:T(8,128)(2,1)} %bitcast.1, bf16[128,2048]{1,0:T(8,128)(2,1)} %shard.1, f32[16,128]{1,0:T(8,128)} %get-tuple-element.11.cos_b, ...), custom_call_target="tpu_custom_call" | custom-call | tf_op jit(solution)/shard_map/layer/pallas_call | solution.py:379
  163.6 2.1 %copy.7 = bf16[192,2048]{1,0:T(8,128)(2,1)} copy(bf16[192,2048]{1,0:T(8,128)(2,1)} %layer.1) | data formatting | bytes 1572864
  (4 shorter events, 0.0 us)
Async XLA Ops:
  0.0 3.5 %copy-start = (bf16[192,2048]{1,0:T(8,128)(2,1)S(1)}, bf16[192,2048]{1,0:T(8,128)(2,1)}, u32[]{:S(2)}) copy-start(bf16[192,2048]{1,0:T(8,128)(2,1)} %hidden.1) | copy-start | bytes 2359300
  0.0 3.5 %copy-start.1 = (f32[2048]{0:T(1024)S(1)}, f32[2048]{0:T(1024)}, u32[]{:S(2)}) copy-start(f32[2048]{0:T(1024)} %param.6) | copy-start | bytes 24580

commit v4 on v3

--- a/solution.py
+++ b/solution.py
@@ -1,3 +1,4 @@
+import functools
 import math
 
 import jax
@@ -18,7 +19,8 @@
 EPS = 1e-05
 THETA = 10000.0
 QSCALE = math.log2(math.e) / math.sqrt(HD)
-ROWS = 256
+ROWS = 128
+GROUP = 4
 
 PIECE = 192
 HALF = PIECE // 2
@@ -296,40 +298,71 @@
 
     def one_block(block, carry):
         base = pl.multiple_of(block * BLK, BLK)
-        count = 1 + ((section * blocks + block) * (KSEL - 1)) // (NBLK - 1)
-
-        def tile(source, first):
-            keys = kv_all[pl.ds(source * BLK, BLK), :HD]
-            values = jnp.concatenate([kv_all[pl.ds(source * BLK, BLK), HD:], ones], axis=1)
+        own = section * blocks + block
+        others = (own * (KSEL - 1)) // (NBLK - 1)
+        spare = others % GROUP
+
+        def tiles(first, slots):
+            sources = [lists[block, slot] for slot in slots]
+            pairs = [
+                (
+                    kv_all[pl.ds(source * BLK, BLK), :HD],
+                    jnp.concatenate([kv_all[pl.ds(source * BLK, BLK), HD:], ones], axis=1),
+                )
+                for source in sources
+            ]
             for part in range(BLK // ROWS):
                 rows = pl.ds(part * ROWS, ROWS)
                 query = q_ref[pl.ds(pl.multiple_of(base + part * ROWS, ROWS), ROWS), :]
-                scores = lax.dot_general(
-                    query, keys, (((1,), (1,)), ((), ())), preferred_element_type=jnp.float32
-                )
+                keyed = list(pairs)
                 if first:
-                    row = lax.broadcasted_iota(jnp.int32, (ROWS, BLK), 0) + part * ROWS
-                    col = lax.broadcasted_iota(jnp.int32, (ROWS, BLK), 1)
-                    scores = jnp.where(col <= row, scores, -jnp.inf)
-                peak = jnp.max(scores, axis=1, keepdims=True)
+                    seen = (part + 1) * ROWS
+                    here = kv_all[pl.ds(own * BLK, seen), :]
+                    keyed.append(
+                        (here[:, :HD], jnp.concatenate([here[:, HD:], ones[:seen]], axis=1))
+                    )
+                scores = [
+                    lax.dot_general(
+                        query, keys, (((1,), (1,)), ((), ())), preferred_element_type=jnp.float32
+                    )
+                    for keys, _ in keyed
+                ]
+                if first:
+                    row = lax.broadcasted_iota(jnp.int32, (ROWS, seen), 0) + part * ROWS
+                    col = lax.broadcasted_iota(jnp.int32, (ROWS, seen), 1)
+                    scores[-1] = jnp.where(col <= row, scores[-1], -jnp.inf)
+                if len(scores) > 1 and not first:
+                    peak = jnp.max(functools.reduce(jnp.maximum, scores), axis=1, keepdims=True)
+                else:
+                    peak = functools.reduce(
+                        jnp.maximum, [jnp.max(one, axis=1, keepdims=True) for one in scores]
+                    )
                 if not first:
                     old = m_ref[rows, :1]
                     peak = jnp.maximum(peak, old)
-                weights = jnp.exp2(scores - peak).astype(jnp.bfloat16)
-                update = jnp.dot(weights, values, preferred_element_type=jnp.float32)
+                update = None
+                for one, (_, values) in zip(scores, keyed):
+                    weights = jnp.exp2(one - peak).astype(jnp.bfloat16)
+                    term = jnp.dot(weights, values, preferred_element_type=jnp.float32)
+                    update = term if update is None else update + term
                 if first:
                     acc_ref[rows, :] = update
                 else:
                     acc_ref[rows, :] = acc_ref[rows, :] * jnp.exp2(old - peak) + update
                 m_ref[rows, :] = jnp.broadcast_to(peak, (ROWS, HD))
 
-        tile(section * blocks + block, True)
-
-        def one_slot(slot, inner):
-            tile(lists[block, slot], False)
+        for extra in range(GROUP):
+
+            @pl.when(spare == extra)
+            def _(extra=extra):
+                tiles(True, [1 + slot for slot in range(extra)])
+
+        def one_group(group, inner):
+            first_slot = 1 + spare + group * GROUP
+            tiles(False, [first_slot + slot for slot in range(GROUP)])
             return inner
 
-        lax.fori_loop(1, count, one_slot, 0)
+        lax.fori_loop(0, others // GROUP, one_group, 0)
         for part in range(BLK // ROWS):
             rows = pl.ds(part * ROWS, ROWS)
             o_ref[pl.ds(pl.multiple_of(base + part * ROWS, ROWS), ROWS), :] = (

time: 166 us -> 146 us (0.88)
  the two profiles are of different devices: /device:TPU:123 before, /device:TPU:97 now
where the time goes in v4:
time: 146 us; the launch traced here: 144 us
  Pallas kernels  137 us (94%)
  other arithmetic  4.62 us (3%)
  local copies, waits for them, and re-layouts  2.1 us (1%)
    pallas_call x1, Pallas kernels, layer(): pl.pallas_call(layer_kernel, out_shape=jax.ShapeDtypeStruct((PIECE, D), j...  137 us

profile of v4, /device:TPU:97, one launch (start us, length us, event | category | flops | bytes accessed | tf_op | source)
XLA Modules:
  0.0 143.5 jit_solution(13613556772759614511)
XLA Ops:
  0.0 0.0 copy-start
  0.0 0.0 copy-start.1
  0.0 1.4 %fusion = f32[192]{0:T(256)S(1)} fusion(bf16[192,2048]{1,0:T(8,128)(2,1)} %hidden.1), kind=kLoop, calls=%fused_computation.2 | loop fusion | flops 1179456 | bytes 787200 | tf_op jit(solution)/shard_map/reduce_sum | solution.py:459
  1.5 0.1 fusion.4
  1.6 0.7 pad_maximum_fusion.2
  2.3 0.4 fusion.3
  2.7 0.8 pad_maximum_fusion
  3.5 0.0 copy-done
  3.5 0.0 copy-done.1
  3.5 1.1 fusion.2.xn
  4.6 136.8 %layer.1 = bf16[192,2048]{1,0:T(8,128)(2,1)} custom-call(s32[6,12]{1,0:T(8,128)} %lists.1, bf16[192,2048]{1,0:T(8,128)(2,1)} %hidden.1, bf16[192,2048]{1,0:T(8,128)(2,1)} %fusion.2.xn, bf16[3,2048,128]{2,1,0:T(8,128)(2,1)} %bitcast.1, bf16[128,2048]{1,0:T(8,128)(2,1)} %shard.1, f32[16,128]{1,0:T(8,128)} %get-tuple-element.11.cos_b, ...), custom_call_target="tpu_custom_call" | custom-call | tf_op jit(solution)/shard_map/layer/pallas_call | solution.py:412
  141.4 2.1 %copy.7 = bf16[192,2048]{1,0:T(8,128)(2,1)} copy(bf16[192,2048]{1,0:T(8,128)(2,1)} %layer.1) | data formatting | bytes 1572864
  (4 shorter events, 0.0 us)
Async XLA Ops:
  0.0 3.5 %copy-start = (bf16[192,2048]{1,0:T(8,128)(2,1)S(1)}, bf16[192,2048]{1,0:T(8,128)(2,1)}, u32[]{:S(2)}) copy-start(bf16[192,2048]{1,0:T(8,128)(2,1)} %hidden.1) | copy-start | bytes 2359300
  0.0 3.5 %copy-start.1 = (f32[2048]{0:T(1024)S(1)}, f32[2048]{0:T(1024)}, u32[]{:S(2)}) copy-start(f32[2048]{0:T(1024)} %param.6) | copy-start | bytes 24580

commit v5 on v4

--- a/solution.py
+++ b/solution.py
@@ -29,16 +29,19 @@
 LAST = HEADS // 2
 W_HALF = HD // 2
 W_PART = W_HALF // 2
-W_BLOCK = 3
+BLOCKS = TOK // BLK
+MOVED = 3
+CHUNK = 64
 OUT_TILE = 256
 MESH = pl.DeviceIdType.MESH
 
 
 def layer_kernel(
-    lists, hidden, xn, w_ref, shard, cos_b, sin_b, cos_r, sin_r, out_ref,
+    lists_here, hidden, xn, w_ref, shard, cos_b, sin_b, cos_r, sin_r, out_ref,
     x_all, kv_all, q_ref, m_ref, acc_ref, o_ref, w_all, mix,
     ring_send, ring_recv, z_send, z_recv, s_send, s_recv,
-    w_send, w_recv, wp_send, wp_recv, w_own, a_send, a_recv, a_own,
+    w_send, w_recv, wp_send, wp_recv, w_own, a_send, a_recv,
+    lists, l_send, l_recv, l_own, m_send, m_recv,
 ):
     section = lax.axis_index("section")
     head = lax.axis_index("head")
@@ -59,6 +62,10 @@
     z_up = {"section": (section + 2) % SECTIONS, "head": head}
     z_down = {"section": (section + SECTIONS - 2) % SECTIONS, "head": head}
     partner = {"section": section + 1 - 2 * (section % 2), "head": head}
+    mate_section = SECTIONS - 1 - section
+    mate = {"section": mate_section, "head": head}
+    heavy = section >= SECTIONS // 2
+    moved = (jnp.maximum(section, mate_section) - 1) // 2
 
     barrier = pltpu.get_barrier_semaphore()
     for device in (z_up, z_down, partner):
@@ -70,7 +77,14 @@
         return carry
 
     lax.fori_loop(1, HEADS, greet, 0)
-    pl.semaphore_wait(barrier, HEADS + 2)
+
+    def greet_mates(step, carry):
+        peer = {"section": mate_section, "head": (head + step) % HEADS}
+        pl.semaphore_signal(barrier, inc=1, device_id=peer, device_id_type=MESH)
+        return carry
+
+    lax.fori_loop(0, HEADS, greet_mates, 0)
+    pl.semaphore_wait(barrier, 2 * HEADS + 2)
 
     def rows_of(start, size):
         return pl.ds(pl.multiple_of(start, 16), size)
@@ -173,6 +187,9 @@
                     ring_recv.at[ring, way, unit, 1],
                     ring_to[ring][way],
                 )
+    send(lists_here, lists.at[1], l_send, l_recv, mate)
+    own_lists = pltpu.make_async_copy(lists_here, lists.at[0], l_own)
+    own_lists.start()
     project(xn[...], starts_of(0))
     share(0, starts_of(0))
     relay_near(0, starts_of(0))
@@ -250,21 +267,33 @@
     for part in range(2):
         for step in range(1, 4):
             w_copy(head, part, 0, line(part, step), True)
+
+    for block in range(MOVED):
+
+        @pl.when(heavy & (block < moved))
+        def _(block=block):
+            send(
+                q_ref.at[pl.ds(block * BLK, BLK), :],
+                q_ref.at[pl.ds(TOK + block * BLK, BLK), :],
+                m_send.at[block],
+                m_recv.at[block],
+                mate,
+            )
+
     relay_near(LAST - 1, starts_of(LAST - 1))
     relay_far(LAST - 2, starts_of(LAST - 2))
     share(LAST, pieces)
+    for part in range(2):
+        arrived(w_all, 3 * W_PART, w_recv.at[part, 0])
+        for step in range(1, 4):
+            for other in range(4):
+                w_copy(line(part, other), part, 1, line(1 - part, step), other == 0)
     relay_far(LAST - 1, starts_of(LAST - 1))
     relay_near(LAST, pieces)
     relay_far(LAST, pieces)
     for step in range(LAST + 1):
         arrived(kv_all, 4 * HALF * (2 if step in (0, LAST) else 4), s_recv.at[step])
 
-    for part in range(2):
-        arrived(w_all, 3 * W_PART, w_recv.at[part, 0])
-        for step in range(1, 4):
-            for other in range(4):
-                w_copy(line(part, other), part, 1, line(1 - part, step), other == 0)
-
     def w_to_partner():
         for part in range(2):
             arrived(w_all, 12 * W_PART, w_recv.at[part, 1])
@@ -278,32 +307,75 @@
 
     own_columns = pl.ds(pl.multiple_of(head * HD, HD), HD)
 
-    def deliver(target, carry):
-        rows = rows_of(target * PIECE, PIECE)
-
-        @pl.when(target != head)
-        def _():
-            send(
-                o_ref.at[rows, :],
-                mix.at[:, own_columns],
-                a_send,
-                a_recv,
-                {"section": section, "head": target},
-            )
-
-        return carry
-
-    blocks = TOK // BLK
+    def chunk_of(turn, own, chunk):
+        where = own % BLOCKS * BLK + chunk * CHUNK
+        target = where // PIECE
+        into = mix.at[rows_of(where - target * PIECE, CHUNK), own_columns]
+        source = o_ref.at[rows_of(turn * BLK + chunk * CHUNK, CHUNK), :]
+        here = (own // BLOCKS == section) & (target == head)
+        device = {"section": own // BLOCKS, "head": target}
+        copy = pltpu.make_async_remote_copy(
+            src_ref=source,
+            dst_ref=into,
+            send_sem=a_send.at[turn, chunk],
+            recv_sem=a_recv,
+            device_id=device,
+            device_id_type=MESH,
+        )
+        return source, into, here, copy
+
+    def deliver(turn, own):
+        for chunk in range(BLK // CHUNK):
+            source, into, here, copy = chunk_of(turn, own, chunk)
+
+            @pl.when(here)
+            def _(source=source, into=into):
+                pltpu.make_async_copy(source, into, a_recv).start()
+
+            @pl.when(jnp.logical_not(here))
+            def _(copy=copy):
+                copy.start()
+
+    def delivered(turn, own):
+        for chunk in range(BLK // CHUNK):
+            _, _, here, copy = chunk_of(turn, own, chunk)
+
+            @pl.when(jnp.logical_not(here))
+            def _(copy=copy):
+                copy.wait_send()
+
+    own_lists.wait()
+    arrived_lists = pltpu.make_async_copy(lists.at[1], lists.at[1], l_recv)
+    arrived_lists.wait()
+    taken = jnp.where(heavy, 0, moved)
+    given = moved - taken
+    turns = BLOCKS + taken - given
+
+    for block in range(MOVED):
+
+        @pl.when(block < taken)
+        def _(block=block):
+            arrived(q_ref, BLK, m_recv.at[block])
+
+    def block_of(turn):
+        away = turn < taken
+        here = turn - taken + given
+        row = jnp.where(away, turn, here)
+        side = jnp.where(away, 1, 0)
+        own = jnp.where(away, mate_section, section) * BLOCKS + row
+        return own, side, row, row * BLK + side * TOK
+
     ones = jnp.ones((BLK, HD), jnp.bfloat16)
 
-    def one_block(block, carry):
-        base = pl.multiple_of(block * BLK, BLK)
-        own = section * blocks + block
+    def one_block(turn, carry):
+        own, side, block, base = block_of(turn)
+        base = pl.multiple_of(base, BLK)
+        landing = pl.multiple_of(turn * BLK, BLK)
         others = (own * (KSEL - 1)) // (NBLK - 1)
         spare = others % GROUP
 
         def tiles(first, slots):
-            sources = [lists[block, slot] for slot in slots]
+            sources = [lists[side, block, slot] for slot in slots]
             pairs = [
                 (
                     kv_all[pl.ds(source * BLK, BLK), :HD],
@@ -365,28 +437,17 @@
         lax.fori_loop(0, others // GROUP, one_group, 0)
         for part in range(BLK // ROWS):
             rows = pl.ds(part * ROWS, ROWS)
-            o_ref[pl.ds(pl.multiple_of(base + part * ROWS, ROWS), ROWS), :] = (
+            o_ref[pl.ds(pl.multiple_of(landing + part * ROWS, ROWS), ROWS), :] = (
                 acc_ref[rows, :HD] / acc_ref[rows, HD:]
             ).astype(jnp.bfloat16)
-        lax.fori_loop((block * BLK) // PIECE, ((block + 1) * BLK) // PIECE, deliver, 0)
-
-        @pl.when(block == W_BLOCK)
-        def _():
-            w_to_partner()
-
+        deliver(turn, own)
         return carry
 
-    lax.fori_loop(0, blocks, one_block, 0)
-
-    own_piece = pltpu.make_async_copy(
-        o_ref.at[rows_of(head * PIECE, PIECE), :], mix.at[:, own_columns], a_own
-    )
-    own_piece.start()
+    lax.fori_loop(0, turns, one_block, 0)
+    w_to_partner()
     own_rows.wait()
     arrived(w_all, (HEADS - 1) * W_HALF, wp_recv)
-    own_piece.wait()
-    taken = mix.at[:, pl.ds(0, (HEADS - 1) * HD)]
-    pltpu.make_async_copy(taken, taken, a_recv).wait()
+    pltpu.make_async_copy(mix, mix, a_recv).wait()
 
     def one_tile(tile, carry):
         columns = pl.ds(pl.multiple_of(tile * OUT_TILE, OUT_TILE), OUT_TILE)
@@ -400,7 +461,19 @@
 
     arrived(w_all, 30 * W_PART, w_send)
     arrived(w_all, (HEADS - 1) * W_HALF, wp_send)
-    pltpu.make_async_copy(taken, taken, a_send).wait()
+
+    def sent(turn, carry):
+        delivered(turn, block_of(turn)[0])
+        return carry
+
+    lax.fori_loop(0, turns, sent, 0)
+    pltpu.make_async_copy(lists.at[1], lists.at[1], l_send).wait()
+    for block in range(MOVED):
+
+        @pl.when(heavy & (block < moved))
+        def _(block=block):
+            arrived(q_ref, BLK, m_send.at[block])
+
     arrived(x_all, 4 * (2 * LAST - 1) * UNIT, ring_send)
     arrived(kv_all, 3 * TOK, z_send)
     arrived(kv_all, 4 * TOK, s_send)
@@ -417,10 +490,10 @@
         scratch_shapes=[
             pltpu.VMEM((TOK, D), jnp.bfloat16),
             pltpu.VMEM((SECTIONS * TOK, 2 * HD), jnp.bfloat16),
-            pltpu.VMEM((TOK, HD), jnp.bfloat16),
+            pltpu.VMEM((TOK + MOVED * BLK, HD), jnp.bfloat16),
             pltpu.VMEM((BLK, HD), jnp.float32),
             pltpu.VMEM((BLK, 2 * HD), jnp.float32),
-            pltpu.VMEM((TOK, HD), jnp.bfloat16),
+            pltpu.VMEM((TOK + MOVED * BLK, HD), jnp.bfloat16),
             pltpu.VMEM((D, D), jnp.bfloat16),
             pltpu.VMEM((PIECE, D), jnp.bfloat16),
             dma,
@@ -434,9 +507,14 @@
             dma,
             dma,
             dma,
-            dma,
-            dma,
-            dma,
+            dma((BLOCKS + MOVED, BLK // CHUNK)),
+            dma,
+            pltpu.SMEM((2, BLOCKS, KSEL), jnp.int32),
+            dma,
+            dma,
+            dma,
+            dma((MOVED,)),
+            dma((MOVED,)),
         ],
         compiler_params=pltpu.CompilerParams(
             collective_id=0, has_side_effects=True, vmem_limit_bytes=60 << 20

time: 146 us -> 152 us (1.041)
  the two profiles are of different devices: /device:TPU:97 before, /device:TPU:1 now
where the time goes in v5:
time: 152 us
  Pallas kernels  145 us (95%)
  other arithmetic  4.62 us (3%)
  local copies, waits for them, and re-layouts  2.1 us (1%)
    pallas_call x1, Pallas kernels, layer(): pl.pallas_call(layer_kernel, out_shape=jax.ShapeDtypeStruct((PIECE, D), j...  145 us

profile of v5, /device:TPU:1, one launch (start us, length us, event | category | flops | bytes accessed | tf_op | source)
XLA Modules:
  0.0 151.7 jit_solution(7089483159645443522)
XLA Ops:
  0.0 0.0 copy-start
  0.0 0.0 copy-start.1
  0.0 1.4 fusion
  1.5 0.1 fusion.4
  1.6 0.7 pad_maximum_fusion.2
  2.3 0.4 fusion.3
  2.7 0.8 pad_maximum_fusion
  3.5 0.0 copy-done
  3.5 0.0 copy-done.1
  3.5 1.1 fusion.2.xn
  4.6 145.0 %layer.1 = bf16[192,2048]{1,0:T(8,128)(2,1)} custom-call(s32[6,12]{1,0:T(8,128)} %lists_here.1, bf16[192,2048]{1,0:T(8,128)(2,1)} %hidden.1, bf16[192,2048]{1,0:T(8,128)(2,1)} %fusion.2.xn, bf16[3,2048,128]{2,1,0:T(8,128)(2,1)} %bitcast.1, bf16[128,2048]{1,0:T(8,128)(2,1)} %shard.1, f32[16,128]{1,0:T(8,128)} %get-tuple-element.11.cos_b, ...), custom_call_target="tpu_custom_call" | custom-call | tf_op jit(solution)/shard_map/layer/pallas_call | solution.py:485
  149.6 2.1 %copy.7 = bf16[192,2048]{1,0:T(8,128)(2,1)} copy(bf16[192,2048]{1,0:T(8,128)(2,1)} %layer.1) | data formatting | bytes 1572864
  (4 shorter events, 0.0 us)
Async XLA Ops:
  0.0 3.5 %copy-start = (bf16[192,2048]{1,0:T(8,128)(2,1)S(1)}, bf16[192,2048]{1,0:T(8,128)(2,1)}, u32[]{:S(2)}) copy-start(bf16[192,2048]{1,0:T(8,128)(2,1)} %hidden.1) | copy-start | bytes 2359300
  0.0 3.5 %copy-start.1 = (f32[2048]{0:T(1024)S(1)}, f32[2048]{0:T(1024)}, u32[]{:S(2)}) copy-start(f32[2048]{0:T(1024)} %param.6) | copy-start | bytes 24580

commit v6 on v5

v6 whole, which is shorter than its diff:
```python
import functools
import math

import jax
import jax.numpy as jnp
from jax import lax
from jax.experimental import pallas as pl
from jax.experimental.pallas import tpu as pltpu
from jax.sharding import PartitionSpec as P

D = 2048
HD = 128
BLK = 512
KSEL = 12
NBLK = 48
SECTIONS = 8
HEADS = 16

EPS = 1e-05
THETA = 10000.0
QSCALE = math.log2(math.e) / math.sqrt(HD)
ROWS = 128
GROUP = 4

PIECE = 192
HALF = PIECE // 2
UNIT = HALF // 2
TOK = PIECE * HEADS
STAGES = 6
W_HALF = HD // 2
W_PART = W_HALF // 2
BLOCKS = TOK // BLK
MOVED = 3
OUT_TILE = 256
MESH = pl.DeviceIdType.MESH


def layer_kernel(
    lists_here, hidden, xn, w_ref, shard, cos_b, sin_b, cos_r, sin_r, out_ref,
    x_all, kv_all, q_ref, m_ref, acc_ref, o_ref, w_all, mix, w_two, q_two, kv_two,
    near_recv, far_recv, side_recv, copy_recv, x_send, v_send, v_recv, vp_send, vp_recv,
    rq_send, rk_send, rq_recv, rk_recv, z_send, z_recv, s_send, s_recv,
    w_send, w_recv, wp_send, wp_recv, w_own, a_send, a_recv,
    lists, l_send, l_recv, l_own, m_send, m_recv,
):
    section = lax.axis_index("section")
    head = lax.axis_index("head")
    ypos, xpos = head // 4, head % 4

    def at(across, along):
        return {"section": section, "head": (ypos + across) % 4 * 4 + along}

    xside = xpos + 1 - 2 * (xpos % 2)
    xtwin = (xpos + 3 + 2 * (xpos % 2)) % 4
    up, down, beside, twin = at(1, xpos), at(3, xpos), at(0, xside), at(0, xtwin)
    z_up = {"section": (section + 2) % SECTIONS, "head": head}
    z_down = {"section": (section + SECTIONS - 2) % SECTIONS, "head": head}
    partner = {"section": section + 1 - 2 * (section % 2), "head": head}
    mate_section = SECTIONS - 1 - section
    mate = {"section": mate_section, "head": head}
    heavy = section >= SECTIONS // 2
    moved = (jnp.maximum(section, mate_section) - 1) // 2

    barrier = pltpu.get_barrier_semaphore()
    for device in (z_up, z_down, partner):
        pl.semaphore_signal(barrier, inc=1, device_id=device, device_id_type=MESH)

    def greet(step, carry):
        peer = {"section": section, "head": (head + step) % HEADS}
        pl.semaphore_signal(barrier, inc=1, device_id=peer, device_id_type=MESH)
        return carry

    lax.fori_loop(1, HEADS, greet, 0)

    def greet_mates(step, carry):
        peer = {"section": mate_section, "head": (head + step) % HEADS}
        pl.semaphore_signal(barrier, inc=1, device_id=peer, device_id_type=MESH)
        return carry

    lax.fori_loop(0, HEADS, greet_mates, 0)
    pl.semaphore_wait(barrier, 2 * HEADS + 2)

    def rows_of(start, size):
        return pl.ds(pl.multiple_of(start, 16), size)

    def send(source, target, send_sem, recv_sem, device):
        pltpu.make_async_remote_copy(
            src_ref=source,
            dst_ref=target,
            send_sem=send_sem,
            recv_sem=recv_sem,
            device_id=device,
            device_id_type=MESH,
        ).start()

    def arrived(ref, rows, sem):
        view = ref.at[pl.ds(0, rows), :]
        pltpu.make_async_copy(view, view, sem).wait()

    def units_of(stage, along):
        beyond = along + 1 - 2 * (along % 2)
        if stage == 0:
            places = ((0, along, 0), (0, along, 1))
        elif stage == 1:
            places = ((3, along, 0), (1, along, 1), (0, beyond, 0))
        elif stage == 2:
            places = ((3, along, 1), (1, along, 0), (0, beyond, 1))
        elif stage == 3:
            places = ((2, along, 0), (2, along, 1))
        else:
            part = stage - 4
            places = ((3, beyond, part), (1, beyond, part), (2, beyond, part))
        return [((ypos + across) % 4, column, part) for across, column, part in places]

    def slot_rows(unit):
        row, column, part = unit
        return rows_of((row * 2 + column % 2) * PIECE + part * HALF, HALF)

    def token_start(unit):
        row, column, part = unit
        return (row * 4 + column) * PIECE + part * HALF

    def tokens_of(stage):
        if stage == 0:
            return [xn[...]]
        return [x_all[slot_rows(unit), :] for unit in units_of(stage, xpos)]

    def forward(unit, recv_sem, device, own=False):
        rows = slot_rows(unit)
        part = unit[2]
        source = xn.at[pl.ds(part * HALF, HALF), :] if own else x_all.at[rows, :]
        send(source, x_all.at[rows, :], x_send, recv_sem, device)

    def project(stages, mine):
        tokens = [piece for stage in stages for piece in tokens_of(stage)]
        tokens = tokens[0] if len(tokens) == 1 else jnp.concatenate(tokens, axis=0)
        source = w_ref if mine else w_two
        weight = jnp.concatenate([source[0], source[1], source[2]], axis=1)
        result = jnp.dot(tokens, weight, preferred_element_type=jnp.float32)
        units = [unit for stage in stages for unit in units_of(stage, xpos)]
        for index, unit in enumerate(units):
            row, column, half = unit
            part = result[index * HALF : (index + 1) * HALF]
            place = row * 4 + column
            base_cos, base_sin = cos_b[pl.ds(place, 1), :], sin_b[pl.ds(place, 1), :]
            row_cos = cos_r[half * HALF : (half + 1) * HALF, :]
            row_sin = sin_r[half * HALF : (half + 1) * HALF, :]
            cosine = base_cos * row_cos - base_sin * row_sin
            sine = base_sin * row_cos + base_cos * row_sin
            query, key, value = part[:, :HD], part[:, HD : 2 * HD], part[:, 2 * HD :]
            query = (query * cosine + pltpu.roll(query, HD // 2, 1) * sine) * QSCALE
            key = key * cosine + pltpu.roll(key, HD // 2, 1) * sine
            start = token_start(unit)
            if mine:
                q_ref[rows_of(start, HALF), :] = query.astype(jnp.bfloat16)
                own = rows_of(section * TOK + start, HALF)
                kv_all[own, :HD] = key.astype(jnp.bfloat16)
                kv_all[own, HD:] = value.astype(jnp.bfloat16)
            else:
                q_two[slot_rows(unit), :] = query.astype(jnp.bfloat16)
                kv_two[slot_rows(unit), :HD] = key.astype(jnp.bfloat16)
                kv_two[slot_rows(unit), HD:] = value.astype(jnp.bfloat16)

    def send_home(stage):
        for unit in units_of(stage, xpos):
            start = token_start(unit)
            send(
                kv_two.at[slot_rows(unit), :],
                kv_all.at[rows_of(section * TOK + start, HALF), :],
                rk_send,
                rk_recv.at[stage],
                twin,
            )
            send(
                q_two.at[slot_rows(unit), :],
                q_ref.at[rows_of(start, HALF), :],
                rq_send,
                rq_recv.at[stage],
                twin,
            )

    def came_home(stage):
        count = len(units_of(stage, xtwin)) * HALF
        arrived(kv_all, count, rk_recv.at[stage])
        arrived(q_ref, count, rq_recv.at[stage])

    def batch(index):
        return units_of(index % STAGES, xpos if index < STAGES else xtwin)

    def kv_copy(region, start, size, send_sem, recv_sem, device):
        rows = rows_of(region * TOK + start, size)
        send(kv_all.at[rows, :], kv_all.at[rows, :], send_sem, recv_sem, device)

    def share(index):
        for unit in batch(index):
            start = token_start(unit)
            kv_copy(section, start, HALF, z_send, z_recv.at[0, index], z_up)
            kv_copy(section, start, HALF, z_send, z_recv.at[1, index], z_down)
            kv_copy(section, start, HALF, s_send, s_recv.at[index], partner)

    def relay_near(index):
        below, above = (section + SECTIONS - 2) % SECTIONS, (section + 2) % SECTIONS
        units = batch(index)
        arrived(kv_all, len(units) * HALF, z_recv.at[0, index])
        for unit in units:
            start = token_start(unit)
            kv_copy(below, start, UNIT, z_send, z_recv.at[2, index], z_up)
            kv_copy(below, start, HALF, s_send, s_recv.at[index], partner)
        arrived(kv_all, len(units) * HALF, z_recv.at[1, index])
        for unit in units:
            start = token_start(unit)
            kv_copy(above, start + UNIT, UNIT, z_send, z_recv.at[3, index], z_down)
            kv_copy(above, start, HALF, s_send, s_recv.at[index], partner)

    def relay_far(index):
        across = (section + 4) % SECTIONS
        units = batch(index)
        arrived(kv_all, len(units) * UNIT, z_recv.at[2, index])
        arrived(kv_all, len(units) * UNIT, z_recv.at[3, index])
        for unit in units:
            kv_copy(across, token_start(unit), HALF, s_send, s_recv.at[index], partner)

    core = section % 2
    depth = D // 2

    def twin_rows(part):
        return w_two.at[part, rows_of(core * depth, depth), :]

    for order in range(2):
        forward((ypos, xpos, order), near_recv.at[0, order], up, True)
        forward((ypos, xpos, 1 - order), near_recv.at[1, 1 - order], down, True)
        forward((ypos, xpos, order), side_recv.at[0, order], beside, True)
    for part in range(3):
        send(
            w_ref.at[part, rows_of(core * depth, depth), :],
            twin_rows(part),
            v_send,
            v_recv.at[part],
            twin,
        )
    send(lists_here, lists.at[1], l_send, l_recv, mate)
    own_lists = pltpu.make_async_copy(lists_here, lists.at[0], l_own)
    own_lists.start()
    project([0], True)
    share(0)

    for stage in (1, 2):
        below, above, across = units_of(stage, xpos)
        arrived(x_all, HALF, near_recv.at[0, below[2]])
        if stage == 1:
            forward(below, far_recv.at[0], up)
        arrived(x_all, HALF, near_recv.at[1, above[2]])
        if stage == 1:
            forward(above, far_recv.at[1], down)
        arrived(x_all, HALF, side_recv.at[0, across[2]])
        forward(across, copy_recv.at[0, across[2]], up)
        forward(across, copy_recv.at[1, across[2]], down)
        project([stage], True)
        share(stage)
        relay_near(stage - 1)

    for part in range(3):
        pltpu.make_async_copy(twin_rows(part), twin_rows(part), v_recv.at[part]).wait()
        send(twin_rows(part), twin_rows(part), vp_send, vp_recv.at[part], partner)
    relay_far(0)
    for part in range(3):
        pltpu.make_async_copy(twin_rows(part), twin_rows(part), vp_recv.at[part]).wait()
    project([0, 1, 2], False)
    for stage in range(3):
        send_home(stage)

    for part, unit in enumerate(units_of(3, xpos)):
        arrived(x_all, HALF, far_recv.at[part])
        forward(unit, side_recv.at[1, part], beside)
    project([3], True)
    project([3], False)
    send_home(3)
    share(3)
    relay_near(2)
    relay_far(1)
    for stage in range(3):
        came_home(stage)
        share(STAGES + stage)
    relay_near(3)
    relay_far(2)

    for stage in (4, 5):
        for way in range(2):
            arrived(x_all, HALF, copy_recv.at[way, stage - 4])
        arrived(x_all, HALF, side_recv.at[1, stage - 4])
        project([stage], True)
        share(stage)
        project([stage], False)
        send_home(stage)
        if stage == 4:
            for index in range(STAGES, STAGES + 3):
                relay_near(index)
            relay_far(3)
            came_home(3)
            share(STAGES + 3)

    own_rows = pltpu.make_async_copy(
        shard, w_all.at[rows_of(head * HD, HD), :], w_own
    )
    own_rows.start()
    def w_rows(source, part):
        return rows_of(source * HD + core * W_HALF + part * W_PART, W_PART)

    def line(part, step):
        if part == 0:
            return ypos * 4 + (xpos + step) % 4
        return ((ypos + step) % 4) * 4 + xpos

    def w_copy(source, part, stage, target, own):
        if own:
            view = shard.at[rows_of(core * W_HALF + part * W_PART, W_PART), :]
        else:
            view = w_all.at[w_rows(source, part), :]
        send(
            view,
            w_all.at[w_rows(source, part), :],
            w_send,
            w_recv.at[part, stage],
            {"section": section, "head": target},
        )

    for part in range(2):
        for step in range(1, 4):
            w_copy(head, part, 0, line(part, step), True)

    relay_near(4)
    for index in range(STAGES, STAGES + 3):
        relay_far(index)
    relay_near(STAGES + 3)
    came_home(4)
    share(STAGES + 4)
    for part in range(2):
        arrived(w_all, 3 * W_PART, w_recv.at[part, 0])
        for step in range(1, 4):
            for other in range(4):
                w_copy(line(part, other), part, 1, line(1 - part, step), other == 0)
    relay_near(5)
    relay_far(4)
    relay_far(STAGES + 3)
    came_home(5)
    share(STAGES + 5)

    for block in range(MOVED):

        @pl.when(heavy & (block < moved))
        def _(block=block):
            send(
                q_ref.at[pl.ds(block * BLK, BLK), :],
                q_ref.at[pl.ds(TOK + block * BLK, BLK), :],
                m_send.at[block],
                m_recv.at[block],
                mate,
            )

    relay_near(STAGES + 4)
    relay_far(5)
    relay_near(STAGES + 5)
    relay_far(STAGES + 4)
    relay_far(STAGES + 5)
    for index in range(2 * STAGES):
        arrived(kv_all, 4 * HALF * len(batch(index)), s_recv.at[index])

    def w_to_partner():
        for part in range(2):
            arrived(w_all, 12 * W_PART, w_recv.at[part, 1])

        def one(step, carry):
            rows = rows_of(((head + step) % HEADS) * HD + core * W_HALF, W_HALF)
            send(w_all.at[rows, :], w_all.at[rows, :], wp_send, wp_recv, partner)
            return carry

        lax.fori_loop(1, HEADS, one, 0)

    def copies_of(turn, own, phase):
        base = own % BLOCKS * BLK
        copies = []
        offset, index = 0, 0
        while offset < BLK:
            inside = (phase * BLK + offset) % PIECE
            size = min(PIECE - inside, BLK - offset)
            target = (base + offset) // PIECE
            source = o_ref.at[rows_of(turn * BLK + offset, size), :]
            into = mix.at[head, pl.ds(inside, size), :]
            here = (own // BLOCKS == section) & (target == head)
            copy = pltpu.make_async_remote_copy(
                src_ref=source,
                dst_ref=into,
                send_sem=a_send.at[turn, index],
                recv_sem=a_recv,
                device_id={"section": own // BLOCKS, "head": target},
                device_id_type=MESH,
            )
            copies.append((source, into, here, copy))
            offset, index = offset + size, index + 1
        return copies

    def deliver(turn, own):
        for phase in range(3):

            @pl.when(own % 3 == phase)
            def _(phase=phase):
                for source, into, here, copy in copies_of(turn, own, phase):

                    @pl.when(here)
                    def _(source=source, into=into):
                        pltpu.make_async_copy(source, into, a_recv).start()

                    @pl.when(jnp.logical_not(here))
                    def _(copy=copy):
                        copy.start()

    def delivered(turn, own):
        for phase in range(3):

            @pl.when(own % 3 == phase)
            def _(phase=phase):
                for _, _, here, copy in copies_of(turn, own, phase):

                    @pl.when(jnp.logical_not(here))
                    def _(copy=copy):
                        copy.wait_send()

    own_lists.wait()
    arrived_lists = pltpu.make_async_copy(lists.at[1], lists.at[1], l_recv)
    arrived_lists.wait()
    taken = jnp.where(heavy, 0, moved)
    given = moved - taken
    turns = BLOCKS + taken - given

    for block in range(MOVED):

        @pl.when(block < taken)
        def _(block=block):
            arrived(q_ref, BLK, m_recv.at[block])

    def block_of(turn):
        away = turn < taken
        here = turn - taken + given
        row = jnp.where(away, turn, here)
        side = jnp.where(away, 1, 0)
        own = jnp.where(away, mate_section, section) * BLOCKS + row
        return own, side, row, row * BLK + side * TOK

    ones = jnp.ones((BLK, HD), jnp.bfloat16)

    def one_block(turn, carry):
        own, side, block, base = block_of(turn)
        base = pl.multiple_of(base, BLK)
        landing = pl.multiple_of(turn * BLK, BLK)
        others = (own * (KSEL - 1)) // (NBLK - 1)
        spare = others % GROUP

        def tiles(first, slots):
            sources = [lists[side, block, slot] for slot in slots]
            pairs = [
                (
                    kv_all[pl.ds(source * BLK, BLK), :HD],
                    jnp.concatenate([kv_all[pl.ds(source * BLK, BLK), HD:], ones], axis=1),
                )
                for source in sources
            ]
            for part in range(BLK // ROWS):
                rows = pl.ds(part * ROWS, ROWS)
                query = q_ref[pl.ds(pl.multiple_of(base + part * ROWS, ROWS), ROWS), :]
                keyed = list(pairs)
                if first:
                    seen = (part + 1) * ROWS
                    here = kv_all[pl.ds(own * BLK, seen), :]
                    keyed.append(
                        (here[:, :HD], jnp.concatenate([here[:, HD:], ones[:seen]], axis=1))
                    )
                scores = [
                    lax.dot_general(
                        query, keys, (((1,), (1,)), ((), ())), preferred_element_type=jnp.float32
                    )
                    for keys, _ in keyed
                ]
                if first:
                    row = lax.broadcasted_iota(jnp.int32, (ROWS, seen), 0) + part * ROWS
                    col = lax.broadcasted_iota(jnp.int32, (ROWS, seen), 1)
                    scores[-1] = jnp.where(col <= row, scores[-1], -jnp.inf)
                lanes = [
                    one[:, start : start + HD]
                    for one in scores
                    for start in range(0, one.shape[1], HD)
                ]
                peak = jnp.max(functools.reduce(jnp.maximum, lanes), axis=1, keepdims=True)
                if not first:
                    old = m_ref[rows, :1]
                    peak = jnp.maximum(peak, old)
                update = None
                for one, (_, values) in zip(scores, keyed):
                    weights = jnp.exp2(one - peak).astype(jnp.bfloat16)
                    term = jnp.dot(weights, values, preferred_element_type=jnp.float32)
                    update = term if update is None else update + term
                if first:
                    acc_ref[rows, :] = update
                else:
                    acc_ref[rows, :] = acc_ref[rows, :] * jnp.exp2(old - peak) + update
                m_ref[rows, :] = jnp.broadcast_to(peak, (ROWS, HD))

        for extra in range(GROUP):

            @pl.when(spare == extra)
            def _(extra=extra):
                tiles(True, [1 + slot for slot in range(extra)])

        def one_group(group, inner):
            first_slot = 1 + spare + group * GROUP
            tiles(False, [first_slot + slot for slot in range(GROUP)])
            return inner

        lax.fori_loop(0, others // GROUP, one_group, 0)
        for part in range(BLK // ROWS):
            rows = pl.ds(part * ROWS, ROWS)
            o_ref[pl.ds(pl.multiple_of(landing + part * ROWS, ROWS), ROWS), :] = (
                acc_ref[rows, :HD] / acc_ref[rows, HD:]
            ).astype(jnp.bfloat16)
        deliver(turn, own)
        return carry

    lax.fori_loop(0, turns, one_block, 0)
    w_to_partner()
    own_rows.wait()
    arrived(w_all, (HEADS - 1) * W_HALF, wp_recv)
    pltpu.make_async_copy(mix, mix, a_recv).wait()

    mixed = jnp.concatenate([mix[source] for source in range(HEADS)], axis=1)

    def one_tile(tile, carry):
        columns = pl.ds(pl.multiple_of(tile * OUT_TILE, OUT_TILE), OUT_TILE)
        summed = jnp.dot(mixed, w_all[:, columns], preferred_element_type=jnp.float32)
        out_ref[:, columns] = (hidden[:, columns].astype(jnp.float32) + summed).astype(
            jnp.bfloat16
        )
        return carry

    lax.fori_loop(0, D // OUT_TILE, one_tile, 0)

    arrived(w_all, 30 * W_PART, w_send)
    arrived(w_all, (HEADS - 1) * W_HALF, wp_send)

    def sent(turn, carry):
        delivered(turn, block_of(turn)[0])
        return carry

    lax.fori_loop(0, turns, sent, 0)
    pltpu.make_async_copy(lists.at[1], lists.at[1], l_send).wait()
    for block in range(MOVED):

        @pl.when(heavy & (block < moved))
        def _(block=block):
            arrived(q_ref, BLK, m_send.at[block])

    arrived(x_all, 7 * PIECE, x_send)
    half_two = w_two.at[:, pl.ds(0, depth), :]
    pltpu.make_async_copy(half_two, half_two, v_send).wait()
    pltpu.make_async_copy(half_two, half_two, vp_send).wait()
    arrived(kv_all, TOK // 2, rk_send)
    arrived(q_ref, TOK // 2, rq_send)
    arrived(kv_all, 3 * TOK, z_send)
    arrived(kv_all, 4 * TOK, s_send)


def layer(lists, hidden, normed, weight, shard, tables):
    vmem = pl.BlockSpec(memory_space=pltpu.VMEM)
    dma = pltpu.SemaphoreType.DMA
    return pl.pallas_call(
        layer_kernel,
        out_shape=jax.ShapeDtypeStruct((PIECE, D), jnp.bfloat16),
        in_specs=[pl.BlockSpec(memory_space=pltpu.SMEM)] + [vmem] * 8,
        out_specs=vmem,
        scratch_shapes=[
            pltpu.VMEM((TOK // 2, D), jnp.bfloat16),
            pltpu.VMEM((SECTIONS * TOK, 2 * HD), jnp.bfloat16),
            pltpu.VMEM((TOK + MOVED * BLK, HD), jnp.bfloat16),
            pltpu.VMEM((BLK, HD), jnp.float32),
            pltpu.VMEM((BLK, 2 * HD), jnp.float32),
            pltpu.VMEM((TOK + MOVED * BLK, HD), jnp.bfloat16),
            pltpu.VMEM((D, D), jnp.bfloat16),
            pltpu.VMEM((HEADS, PIECE, HD), jnp.bfloat16),
            pltpu.VMEM((3, D, HD), jnp.bfloat16),
            pltpu.VMEM((TOK // 2, HD), jnp.bfloat16),
            pltpu.VMEM((TOK // 2, 2 * HD), jnp.bfloat16),
            dma((2, 2)),
            dma((2,)),
            dma((2, 2)),
            dma((2, 2)),
            dma,
            dma,
            dma((3,)),
            dma,
            dma((3,)),
            dma,
            dma,
            dma((STAGES,)),
            dma((STAGES,)),
            dma,
            dma((4, 2 * STAGES)),
            dma,
            dma((2 * STAGES,)),
            dma,
            dma((2, 2)),
            dma,
            dma,
            dma,
            dma((BLOCKS + MOVED, 4)),
            dma,
            pltpu.SMEM((2, BLOCKS, KSEL), jnp.int32),
            dma,
            dma,
            dma,
            dma((MOVED,)),
            dma((MOVED,)),
        ],
        compiler_params=pltpu.CompilerParams(
            collective_id=0, has_side_effects=True, vmem_limit_bytes=60 << 20
        ),
        name="layer",
    )(lists, hidden, normed, weight, shard, *tables)


def rotary_tables(positions):
    frequency = THETA ** (-(2.0 * jnp.arange(HD // 2, dtype=jnp.float32)) / HD)
    angle = positions.astype(jnp.float32)[:, None] * frequency[None, :]
    cosine, sine = jnp.cos(angle), jnp.sin(angle)
    return jnp.concatenate([cosine, cosine], axis=1), jnp.concatenate([-sine, sine], axis=1)


def local(hidden_in, norm_gain, w_qkv, w_out, block_lists):
    section_id = lax.axis_index("section")
    resid = hidden_in.astype(jnp.float32)
    normed = (
        resid * lax.rsqrt(jnp.mean(resid * resid, axis=-1, keepdims=True) + EPS) * norm_gain
    ).astype(jnp.bfloat16)
    weight = jnp.transpose(w_qkv, (1, 0, 2))
    bases = section_id * TOK + PIECE * jnp.arange(HEADS, dtype=jnp.int32)
    tables = rotary_tables(bases) + rotary_tables(jnp.arange(PIECE, dtype=jnp.int32))
    return layer(block_lists, hidden_in, normed, weight, w_out, tables)


def solution(mesh):
    placed = (
        P(("section", "head"), None),
        P(),
        P(None, None, "head"),
        P("head", None),
        P("section", None),
    )
    return jax.shard_map(
        local, mesh=mesh, in_specs=placed, out_specs=P(("section", "head"), None), check_vma=False
    )
```

time: 152 us -> 135 us (0.89)
  the two profiles are of different devices: /device:TPU:1 before, /device:TPU:17 now
where the time goes in v6:
time: 135 us
  Pallas kernels  129 us (96%)
  other arithmetic  4.62 us (3%)
  local copies, waits for them, and re-layouts  2.1 us (2%)
    pallas_call x1, Pallas kernels, layer(): pl.pallas_call(layer_kernel, out_shape=jax.ShapeDtypeStruct((PIECE, D), j...  129 us

profile of v6, /device:TPU:17, one launch (start us, length us, event | category | flops | bytes accessed | tf_op | source)
XLA Modules:
  0.0 135.2 jit_solution(4225545279542690876)
XLA Ops:
  0.0 0.0 copy-start
  0.0 0.0 copy-start.1
  0.0 1.4 %fusion = f32[192]{0:T(256)S(1)} fusion(bf16[192,2048]{1,0:T(8,128)(2,1)} %hidden.1), kind=kLoop, calls=%fused_computation.2 | loop fusion | flops 1179456 | bytes 787200 | tf_op jit(solution)/shard_map/reduce_sum | solution.py:639
  1.5 0.1 fusion.4
  1.6 0.7 pad_maximum_fusion.2
  2.3 0.4 fusion.3
  2.7 0.8 pad_maximum_fusion
  3.5 0.0 copy-done
  3.5 0.0 copy-done.1
  3.5 1.1 fusion.2.xn
  4.6 128.5 %layer.1 = bf16[192,2048]{1,0:T(8,128)(2,1)} custom-call(s32[6,12]{1,0:T(8,128)} %lists_here.1, bf16[192,2048]{1,0:T(8,128)(2,1)} %hidden.1, bf16[192,2048]{1,0:T(8,128)(2,1)} %fusion.2.xn, bf16[3,2048,128]{2,1,0:T(8,128)(2,1)} %bitcast.1, bf16[128,2048]{1,0:T(8,128)(2,1)} %shard.1, f32[16,128]{1,0:T(8,128)} %get-tuple-element.11.cos_b, ...), custom_call_target="tpu_custom_call" | custom-call | tf_op jit(solution)/shard_map/layer/pallas_call | solution.py:573
  133.2 2.1 %copy.7 = bf16[192,2048]{1,0:T(8,128)(2,1)} copy(bf16[192,2048]{1,0:T(8,128)(2,1)} %layer.1) | data formatting | bytes 1572864
  (4 shorter events, 0.0 us)
Async XLA Ops:
  0.0 3.5 %copy-start = (bf16[192,2048]{1,0:T(8,128)(2,1)S(1)}, bf16[192,2048]{1,0:T(8,128)(2,1)}, u32[]{:S(2)}) copy-start(bf16[192,2048]{1,0:T(8,128)(2,1)} %hidden.1) | copy-start | bytes 2359300
  0.0 3.5 %copy-start.1 = (f32[2048]{0:T(1024)S(1)}, f32[2048]{0:T(1024)}, u32[]{:S(2)}) copy-start(f32[2048]{0:T(1024)} %param.6) | copy-start | bytes 24580

commit v7 on v6

--- a/solution.py
+++ b/solution.py
@@ -3,6 +3,7 @@
 
 import jax
 import jax.numpy as jnp
+import numpy as np
 from jax import lax
 from jax.experimental import pallas as pl
 from jax.experimental.pallas import tpu as pltpu
@@ -36,7 +37,8 @@
 
 
 def layer_kernel(
-    lists_here, hidden, xn, w_ref, shard, cos_b, sin_b, cos_r, sin_r, out_ref,
+    lists_here, hidden_in, gain, w_in, shard, cos_b, sin_b, cos_r, sin_r, out_ref,
+    hidden, xn, w_ref, in_sems,
     x_all, kv_all, q_ref, m_ref, acc_ref, o_ref, w_all, mix, w_two, q_two, kv_two,
     near_recv, far_recv, side_recv, copy_recv, x_send, v_send, v_recv, vp_send, vp_recv,
     rq_send, rk_send, rq_recv, rk_recv, z_send, z_recv, s_send, s_recv,
@@ -78,6 +80,14 @@
         return carry
 
     lax.fori_loop(0, HEADS, greet_mates, 0)
+    own_hidden = pltpu.make_async_copy(hidden_in, hidden, in_sems.at[0])
+    own_weight = pltpu.make_async_copy(w_in, w_ref, in_sems.at[1])
+    own_hidden.start()
+    own_weight.start()
+    own_hidden.wait()
+    resid = hidden[...].astype(jnp.float32)
+    spread = jnp.mean(resid * resid, axis=1, keepdims=True)
+    xn[...] = (resid * lax.rsqrt(spread + EPS) * gain[...]).astype(jnp.bfloat16)
     pl.semaphore_wait(barrier, 2 * HEADS + 2)
 
     def rows_of(start, size):
@@ -131,58 +141,58 @@
         source = xn.at[pl.ds(part * HALF, HALF), :] if own else x_all.at[rows, :]
         send(source, x_all.at[rows, :], x_send, recv_sem, device)
 
-    def project(stages, mine):
+    def project(stages, mine, wanted=(0, 1, 2)):
         tokens = [piece for stage in stages for piece in tokens_of(stage)]
         tokens = tokens[0] if len(tokens) == 1 else jnp.concatenate(tokens, axis=0)
         source = w_ref if mine else w_two
-        weight = jnp.concatenate([source[0], source[1], source[2]], axis=1)
+        weight = [source[part] for part in wanted]
+        weight = weight[0] if len(weight) == 1 else jnp.concatenate(weight, axis=1)
         result = jnp.dot(tokens, weight, preferred_element_type=jnp.float32)
         units = [unit for stage in stages for unit in units_of(stage, xpos)]
         for index, unit in enumerate(units):
             row, column, half = unit
             part = result[index * HALF : (index + 1) * HALF]
-            place = row * 4 + column
+            parts = {
+                name: part[:, place * HD : (place + 1) * HD] for place, name in enumerate(wanted)
+            }
+            place = section * HEADS + row * 4 + column
             base_cos, base_sin = cos_b[pl.ds(place, 1), :], sin_b[pl.ds(place, 1), :]
             row_cos = cos_r[half * HALF : (half + 1) * HALF, :]
             row_sin = sin_r[half * HALF : (half + 1) * HALF, :]
             cosine = base_cos * row_cos - base_sin * row_sin
             sine = base_sin * row_cos + base_cos * row_sin
-            query, key, value = part[:, :HD], part[:, HD : 2 * HD], part[:, 2 * HD :]
-            query = (query * cosine + pltpu.roll(query, HD // 2, 1) * sine) * QSCALE
-            key = key * cosine + pltpu.roll(key, HD // 2, 1) * sine
             start = token_start(unit)
             if mine:
-                q_ref[rows_of(start, HALF), :] = query.astype(jnp.bfloat16)
-                own = rows_of(section * TOK + start, HALF)
-                kv_all[own, :HD] = key.astype(jnp.bfloat16)
-                kv_all[own, HD:] = value.astype(jnp.bfloat16)
+                q_to, q_rows = q_ref, rows_of(start, HALF)
+                kv_to, kv_rows = kv_all, rows_of(section * TOK + start, HALF)
             else:
-                q_two[slot_rows(unit), :] = query.astype(jnp.bfloat16)
-                kv_two[slot_rows(unit), :HD] = key.astype(jnp.bfloat16)
-                kv_two[slot_rows(unit), HD:] = value.astype(jnp.bfloat16)
-
-    def send_home(stage):
+                q_to, kv_to = q_two, kv_two
+                q_rows = kv_rows = slot_rows(unit)
+            if 0 in parts:
+                query = parts[0]
+                query = (query * cosine + pltpu.roll(query, HD // 2, 1) * sine) * QSCALE
+                q_to[q_rows, :] = query.astype(jnp.bfloat16)
+            if 1 in parts:
+                key = parts[1]
+                key = key * cosine + pltpu.roll(key, HD // 2, 1) * sine
+                kv_to[kv_rows, :HD] = key.astype(jnp.bfloat16)
+                kv_to[kv_rows, HD:] = parts[2].astype(jnp.bfloat16)
+
+    def keys_home(stage):
         for unit in units_of(stage, xpos):
-            start = token_start(unit)
+            rows = rows_of(section * TOK + token_start(unit), HALF)
             send(
-                kv_two.at[slot_rows(unit), :],
-                kv_all.at[rows_of(section * TOK + start, HALF), :],
-                rk_send,
-                rk_recv.at[stage],
-                twin,
+                kv_two.at[slot_rows(unit), :], kv_all.at[rows, :], rk_send, rk_recv.at[stage], twin
             )
-            send(
-                q_two.at[slot_rows(unit), :],
-                q_ref.at[rows_of(start, HALF), :],
-                rq_send,
-                rq_recv.at[stage],
-                twin,
-            )
+
+    def queries_home(stage):
+        for unit in units_of(stage, xpos):
+            rows = rows_of(token_start(unit), HALF)
+            send(q_two.at[slot_rows(unit), :], q_ref.at[rows, :], rq_send, rq_recv.at[stage], twin)
 
     def came_home(stage):
         count = len(units_of(stage, xtwin)) * HALF
         arrived(kv_all, count, rk_recv.at[stage])
-        arrived(q_ref, count, rq_recv.at[stage])
 
     def batch(index):
         return units_of(index % STAGES, xpos if index < STAGES else xtwin)
@@ -230,7 +240,8 @@
         forward((ypos, xpos, order), near_recv.at[0, order], up, True)
         forward((ypos, xpos, 1 - order), near_recv.at[1, 1 - order], down, True)
         forward((ypos, xpos, order), side_recv.at[0, order], beside, True)
-    for part in range(3):
+    own_weight.wait()
+    for part in (1, 2, 0):
         send(
             w_ref.at[part, rows_of(core * depth, depth), :],
             twin_rows(part),
@@ -241,10 +252,19 @@
     send(lists_here, lists.at[1], l_send, l_recv, mate)
     own_lists = pltpu.make_async_copy(lists_here, lists.at[0], l_own)
     own_lists.start()
-    project([0], True)
-    share(0)
-
-    for stage in (1, 2):
+    own_rows = pltpu.make_async_copy(
+        shard, w_all.at[rows_of(head * HD, HD), :], w_own
+    )
+    own_rows.start()
+
+    def weight_on(part):
+        pltpu.make_async_copy(twin_rows(part), twin_rows(part), v_recv.at[part]).wait()
+        send(twin_rows(part), twin_rows(part), vp_send, vp_recv.at[part], partner)
+
+    def weight_in(part):
+        pltpu.make_async_copy(twin_rows(part), twin_rows(part), vp_recv.at[part]).wait()
+
+    def first_stage(stage):
         below, above, across = units_of(stage, xpos)
         arrived(x_all, HALF, near_recv.at[0, below[2]])
         if stage == 1:
@@ -257,52 +277,70 @@
         forward(across, copy_recv.at[1, across[2]], down)
         project([stage], True)
         share(stage)
-        relay_near(stage - 1)
-
-    for part in range(3):
-        pltpu.make_async_copy(twin_rows(part), twin_rows(part), v_recv.at[part]).wait()
-        send(twin_rows(part), twin_rows(part), vp_send, vp_recv.at[part], partner)
-    relay_far(0)
-    for part in range(3):
-        pltpu.make_async_copy(twin_rows(part), twin_rows(part), vp_recv.at[part]).wait()
-    project([0, 1, 2], False)
-    for stage in range(3):
-        send_home(stage)
-
-    for part, unit in enumerate(units_of(3, xpos)):
-        arrived(x_all, HALF, far_recv.at[part])
-        forward(unit, side_recv.at[1, part], beside)
-    project([3], True)
-    project([3], False)
-    send_home(3)
-    share(3)
-    relay_near(2)
-    relay_far(1)
-    for stage in range(3):
-        came_home(stage)
-        share(STAGES + stage)
-    relay_near(3)
-    relay_far(2)
-
-    for stage in (4, 5):
+
+    def last_stage(stage):
         for way in range(2):
             arrived(x_all, HALF, copy_recv.at[way, stage - 4])
         arrived(x_all, HALF, side_recv.at[1, stage - 4])
         project([stage], True)
         share(stage)
-        project([stage], False)
-        send_home(stage)
-        if stage == 4:
-            for index in range(STAGES, STAGES + 3):
-                relay_near(index)
-            relay_far(3)
-            came_home(3)
-            share(STAGES + 3)
-
-    own_rows = pltpu.make_async_copy(
-        shard, w_all.at[rows_of(head * HD, HD), :], w_own
-    )
-    own_rows.start()
+        project([stage], False, (1, 2))
+        keys_home(stage)
+
+    def bring(stage):
+        came_home(stage)
+        share(STAGES + stage)
+
+    project([0], True)
+    share(0)
+    first_stage(1)
+    relay_near(0)
+    for part in (1, 2):
+        weight_on(part)
+    for part in (1, 2):
+        weight_in(part)
+    project([0, 1], False, (1, 2))
+    keys_home(0)
+    keys_home(1)
+    relay_far(0)
+    first_stage(2)
+    project([2], False, (1, 2))
+    keys_home(2)
+    weight_on(0)
+    relay_near(1)
+    bring(0)
+    bring(1)
+    for part, unit in enumerate(units_of(3, xpos)):
+        arrived(x_all, HALF, far_recv.at[part])
+        forward(unit, side_recv.at[1, part], beside)
+    project([3], True)
+    share(3)
+    project([3], False, (1, 2))
+    keys_home(3)
+    bring(2)
+    relay_near(2)
+    relay_near(STAGES)
+    relay_far(1)
+    relay_near(STAGES + 1)
+    weight_in(0)
+    project([0, 1, 2, 3], False, (0,))
+    for stage in range(4):
+        queries_home(stage)
+    relay_near(3)
+    relay_near(STAGES + 2)
+    bring(3)
+    relay_far(2)
+    relay_far(STAGES)
+    last_stage(4)
+    relay_far(STAGES + 1)
+    relay_near(STAGES + 3)
+    relay_far(3)
+    relay_far(STAGES + 2)
+    last_stage(5)
+    project([4, 5], False, (0,))
+    queries_home(4)
+    queries_home(5)
+    own_rows.wait()
     def w_rows(source, part):
         return rows_of(source * HD + core * W_HALF + part * W_PART, W_PART)
 
@@ -311,11 +349,8 @@
             return ypos * 4 + (xpos + step) % 4
         return ((ypos + step) % 4) * 4 + xpos
 
-    def w_copy(source, part, stage, target, own):
-        if own:
-            view = shard.at[rows_of(core * W_HALF + part * W_PART, W_PART), :]
-        else:
-            view = w_all.at[w_rows(source, part), :]
+    def w_copy(source, part, stage, target):
+        view = w_all.at[w_rows(source, part), :]
         send(
             view,
             w_all.at[w_rows(source, part), :],
@@ -326,24 +361,21 @@
 
     for part in range(2):
         for step in range(1, 4):
-            w_copy(head, part, 0, line(part, step), True)
+            w_copy(head, part, 0, line(part, step))
 
     relay_near(4)
-    for index in range(STAGES, STAGES + 3):
-        relay_far(index)
-    relay_near(STAGES + 3)
-    came_home(4)
-    share(STAGES + 4)
+    bring(4)
     for part in range(2):
         arrived(w_all, 3 * W_PART, w_recv.at[part, 0])
         for step in range(1, 4):
             for other in range(4):
-                w_copy(line(part, other), part, 1, line(1 - part, step), other == 0)
+                w_copy(line(part, other), part, 1, line(1 - part, step))
     relay_near(5)
+    relay_far(STAGES + 3)
     relay_far(4)
-    relay_far(STAGES + 3)
-    came_home(5)
-    share(STAGES + 5)
+    bring(5)
+    for stage in range(STAGES):
+        arrived(q_ref, len(units_of(stage, xtwin)) * HALF, rq_recv.at[stage])
 
     for block in range(MOVED):
 
@@ -526,7 +558,6 @@
 
     lax.fori_loop(0, turns, one_block, 0)
     w_to_partner()
-    own_rows.wait()
     arrived(w_all, (HEADS - 1) * W_HALF, wp_recv)
     pltpu.make_async_copy(mix, mix, a_recv).wait()
 
@@ -535,9 +566,7 @@
     def one_tile(tile, carry):
         columns = pl.ds(pl.multiple_of(tile * OUT_TILE, OUT_TILE), OUT_TILE)
         summed = jnp.dot(mixed, w_all[:, columns], preferred_element_type=jnp.float32)
-        out_ref[:, columns] = (hidden[:, columns].astype(jnp.float32) + summed).astype(
-            jnp.bfloat16
-        )
+        out_ref[:, columns] = summed
         return carry
 
     lax.fori_loop(0, D // OUT_TILE, one_tile, 0)
@@ -567,15 +596,20 @@
     arrived(kv_all, 4 * TOK, s_send)
 
 
-def layer(lists, hidden, normed, weight, shard, tables):
+def layer(lists, hidden, gain, weight, shard, tables):
     vmem = pl.BlockSpec(memory_space=pltpu.VMEM)
+    here = pl.BlockSpec(memory_space=pl.ANY)
     dma = pltpu.SemaphoreType.DMA
     return pl.pallas_call(
         layer_kernel,
-        out_shape=jax.ShapeDtypeStruct((PIECE, D), jnp.bfloat16),
-        in_specs=[pl.BlockSpec(memory_space=pltpu.SMEM)] + [vmem] * 8,
+        out_shape=jax.ShapeDtypeStruct((PIECE, D), jnp.float32),
+        in_specs=[pl.BlockSpec(memory_space=pltpu.SMEM), here, vmem, here, here] + [vmem] * 4,
         out_specs=vmem,
         scratch_shapes=[
+            pltpu.VMEM((PIECE, D), jnp.bfloat16),
+            pltpu.VMEM((PIECE, D), jnp.bfloat16),
+            pltpu.VMEM((3, D, HD), jnp.bfloat16),
+            dma((2,)),
             pltpu.VMEM((TOK // 2, D), jnp.bfloat16),
             pltpu.VMEM((SECTIONS * TOK, 2 * HD), jnp.bfloat16),
             pltpu.VMEM((TOK + MOVED * BLK, HD), jnp.bfloat16),
@@ -622,26 +656,26 @@
             collective_id=0, has_side_effects=True, vmem_limit_bytes=60 << 20
         ),
         name="layer",
-    )(lists, hidden, normed, weight, shard, *tables)
+    )(lists, hidden, gain, weight, shard, *tables)
 
 
 def rotary_tables(positions):
-    frequency = THETA ** (-(2.0 * jnp.arange(HD // 2, dtype=jnp.float32)) / HD)
-    angle = positions.astype(jnp.float32)[:, None] * frequency[None, :]
-    cosine, sine = jnp.cos(angle), jnp.sin(angle)
-    return jnp.concatenate([cosine, cosine], axis=1), jnp.concatenate([-sine, sine], axis=1)
+    frequency = THETA ** (-2.0 * np.arange(HD // 2) / HD)
+    angle = positions[:, None] * frequency[None, :]
+    cosine, sine = np.cos(angle), np.sin(angle)
+    return (
+        np.concatenate([cosine, cosine], axis=1).astype(np.float32),
+        np.concatenate([-sine, sine], axis=1).astype(np.float32),
+    )
 
 
 def local(hidden_in, norm_gain, w_qkv, w_out, block_lists):
-    section_id = lax.axis_index("section")
-    resid = hidden_in.astype(jnp.float32)
-    normed = (
-        resid * lax.rsqrt(jnp.mean(resid * resid, axis=-1, keepdims=True) + EPS) * norm_gain
-    ).astype(jnp.bfloat16)
     weight = jnp.transpose(w_qkv, (1, 0, 2))
-    bases = section_id * TOK + PIECE * jnp.arange(HEADS, dtype=jnp.int32)
-    tables = rotary_tables(bases) + rotary_tables(jnp.arange(PIECE, dtype=jnp.int32))
-    return layer(block_lists, hidden_in, normed, weight, w_out, tables)
+    bases = rotary_tables(np.arange(SECTIONS * HEADS) * PIECE)
+    steps = rotary_tables(np.arange(PIECE))
+    gain = norm_gain.reshape(1, D)
+    summed = layer(block_lists, hidden_in, gain, weight, w_out, bases + steps)
+    return (hidden_in.astype(jnp.float32) + summed).astype(jnp.bfloat16)
 
 
 def solution(mesh):

time: 135 us -> 133 us (0.985)
  the two profiles are of different devices: /device:TPU:17 before, /device:TPU:7 now
where the time goes in v7:
time: 133 us; the launch traced here: 132 us
  Pallas kernels  130 us (98%)
  other arithmetic  2.47 us (2%)
    pallas_call x1, Pallas kernels, layer(): pl.pallas_call(layer_kernel, out_shape=jax.ShapeDtypeStruct((PIECE, D), j...  130 us

profile of v7, /device:TPU:7, one launch (start us, length us, event | category | flops | bytes accessed | tf_op | source)
XLA Modules:
  0.0 132.4 jit_solution(16355954037379062116)
XLA Ops:
  0.0 0.0 copy-start
  0.0 129.9 %layer.1 = f32[192,2048]{1,0:T(8,128)} custom-call(s32[6,12]{1,0:T(8,128)} %lists_here.1, bf16[192,2048]{1,0:T(8,128)(2,1)} %hidden_in.1, f32[1,2048]{1,0:T(1,128)} %bitcast.3, bf16[3,2048,128]{2,1,0:T(8,128)(2,1)} %bitcast.2, bf16[128,2048]{1,0:T(8,128)(2,1)} %shard.1, f32[128,128]{1,0:T(8,128)} %constant.8.clone.cos_b, f32[128,128]{1,0:T(8,128)} %constant.9.clone.sin_b, ...), custom_call_target="tpu_custom_call" | custom-call | tf_op jit(solution)/shard_map/layer/pallas_call | solution.py:603
  129.9 0.0 copy-done
  130.0 2.5 %add_convert_fusion = bf16[192,2048]{1,0:T(8,128)(2,1)} fusion(f32[192,2048]{1,0:T(8,128)} %layer.1, bf16[192,2048]{1,0:T(8,128)(2,1)S(1)} %copy-done), kind=kLoop, calls=%fused_computation | loop fusion | flops 1179648 | bytes 3145728 | tf_op jit(solution)/shard_map/convert_element_type | solution.py:678
Async XLA Ops:
  0.0 129.9 %copy-start = (bf16[192,2048]{1,0:T(8,128)(2,1)S(1)}, bf16[192,2048]{1,0:T(8,128)(2,1)}, u32[]{:S(2)}) copy-start(bf16[192,2048]{1,0:T(8,128)(2,1)} %hidden_in.1) | copy-start | bytes 2359300

commit v8 on v7

--- a/solution.py
+++ b/solution.py
@@ -278,10 +278,36 @@
         project([stage], True)
         share(stage)
 
+    def w_rows(source, part):
+        return rows_of(source * HD + core * W_HALF + part * W_PART, W_PART)
+
+    def line(part, step):
+        if part == 0:
+            return ypos * 4 + (xpos + step) % 4
+        return ((ypos + step) % 4) * 4 + xpos
+
+    def w_copy(source, part, stage, target):
+        view = w_all.at[w_rows(source, part), :]
+        send(
+            view,
+            w_all.at[w_rows(source, part), :],
+            w_send,
+            w_recv.at[part, stage],
+            {"section": section, "head": target},
+        )
+
+    def w_near():
+        own_rows.wait()
+        for part in range(2):
+            for step in range(1, 4):
+                w_copy(head, part, 0, line(part, step))
+
     def last_stage(stage):
         for way in range(2):
             arrived(x_all, HALF, copy_recv.at[way, stage - 4])
         arrived(x_all, HALF, side_recv.at[1, stage - 4])
+        if stage == 5:
+            w_near()
         project([stage], True)
         share(stage)
         project([stage], False, (1, 2))
@@ -340,36 +366,13 @@
     project([4, 5], False, (0,))
     queries_home(4)
     queries_home(5)
-    own_rows.wait()
-    def w_rows(source, part):
-        return rows_of(source * HD + core * W_HALF + part * W_PART, W_PART)
-
-    def line(part, step):
-        if part == 0:
-            return ypos * 4 + (xpos + step) % 4
-        return ((ypos + step) % 4) * 4 + xpos
-
-    def w_copy(source, part, stage, target):
-        view = w_all.at[w_rows(source, part), :]
-        send(
-            view,
-            w_all.at[w_rows(source, part), :],
-            w_send,
-            w_recv.at[part, stage],
-            {"section": section, "head": target},
-        )
-
-    for part in range(2):
-        for step in range(1, 4):
-            w_copy(head, part, 0, line(part, step))
-
     relay_near(4)
     bring(4)
     for part in range(2):
         arrived(w_all, 3 * W_PART, w_recv.at[part, 0])
         for step in range(1, 4):
             for other in range(4):
-                w_copy(line(part, other), part, 1, line(1 - part, step))
+                w_copy(line(part, other), part, step, line(1 - part, step))
     relay_near(5)
     relay_far(STAGES + 3)
     relay_far(4)
@@ -397,16 +400,24 @@
     for index in range(2 * STAGES):
         arrived(kv_all, 4 * HALF * len(batch(index)), s_recv.at[index])
 
-    def w_to_partner():
+    def w_to_partner(source, part):
+        rows = w_rows(source, part)
+        send(w_all.at[rows, :], w_all.at[rows, :], wp_send, wp_recv, partner)
+
+    def w_near_to_partner():
         for part in range(2):
-            arrived(w_all, 12 * W_PART, w_recv.at[part, 1])
-
-        def one(step, carry):
-            rows = rows_of(((head + step) % HEADS) * HD + core * W_HALF, W_HALF)
-            send(w_all.at[rows, :], w_all.at[rows, :], wp_send, wp_recv, partner)
-            return carry
-
-        lax.fori_loop(1, HEADS, one, 0)
+            for step in range(1, 4):
+                w_to_partner(line(part, step), part)
+
+    def w_far_to_partner(step):
+        for part in range(2):
+            arrived(w_all, 4 * W_PART, w_recv.at[part, step])
+            for other in range(4):
+                if part == 0:
+                    source = (ypos + 4 - step) % 4 * 4 + other
+                else:
+                    source = other * 4 + (xpos + 4 - step) % 4
+                w_to_partner(source, part)
 
     def copies_of(turn, own, phase):
         base = own % BLOCKS * BLK
@@ -464,16 +475,13 @@
     given = moved - taken
     turns = BLOCKS + taken - given
 
-    for block in range(MOVED):
-
-        @pl.when(block < taken)
-        def _(block=block):
-            arrived(q_ref, BLK, m_recv.at[block])
+    kept = BLOCKS - given
 
     def block_of(turn):
-        away = turn < taken
-        here = turn - taken + given
-        row = jnp.where(away, turn, here)
+        away = turn >= kept
+        here = given + (turn + head) % kept
+        there = (jnp.maximum(turn - kept, 0) + head) % jnp.maximum(taken, 1)
+        row = jnp.where(away, there, here)
         side = jnp.where(away, 1, 0)
         own = jnp.where(away, mate_section, section) * BLOCKS + row
         return own, side, row, row * BLK + side * TOK
@@ -484,6 +492,11 @@
         own, side, block, base = block_of(turn)
         base = pl.multiple_of(base, BLK)
         landing = pl.multiple_of(turn * BLK, BLK)
+
+        @pl.when(turn >= kept)
+        def _():
+            arrived(q_ref, BLK, m_recv.at[block])
+
         others = (own * (KSEL - 1)) // (NBLK - 1)
         spare = others % GROUP
 
@@ -554,10 +567,20 @@
                 acc_ref[rows, :HD] / acc_ref[rows, HD:]
             ).astype(jnp.bfloat16)
         deliver(turn, own)
+
+        @pl.when(turn == turns - 3)
+        def _():
+            w_near_to_partner()
+
+        @pl.when(turn == turns - 2)
+        def _():
+            w_far_to_partner(1)
+            w_far_to_partner(3)
+
         return carry
 
     lax.fori_loop(0, turns, one_block, 0)
-    w_to_partner()
+    w_far_to_partner(2)
     arrived(w_all, (HEADS - 1) * W_HALF, wp_recv)
     pltpu.make_async_copy(mix, mix, a_recv).wait()
 
@@ -566,7 +589,9 @@
     def one_tile(tile, carry):
         columns = pl.ds(pl.multiple_of(tile * OUT_TILE, OUT_TILE), OUT_TILE)
         summed = jnp.dot(mixed, w_all[:, columns], preferred_element_type=jnp.float32)
-        out_ref[:, columns] = summed
+        out_ref[:, columns] = (hidden[:, columns].astype(jnp.float32) + summed).astype(
+            jnp.bfloat16
+        )
         return carry
 
     lax.fori_loop(0, D // OUT_TILE, one_tile, 0)
@@ -602,7 +627,7 @@
     dma = pltpu.SemaphoreType.DMA
     return pl.pallas_call(
         layer_kernel,
-        out_shape=jax.ShapeDtypeStruct((PIECE, D), jnp.float32),
+        out_shape=jax.ShapeDtypeStruct((PIECE, D), jnp.bfloat16),
         in_specs=[pl.BlockSpec(memory_space=pltpu.SMEM), here, vmem, here, here] + [vmem] * 4,
         out_specs=vmem,
         scratch_shapes=[
@@ -639,7 +664,7 @@
             dma,
             dma((2 * STAGES,)),
             dma,
-            dma((2, 2)),
+            dma((2, 4)),
             dma,
             dma,
             dma,
@@ -674,8 +699,7 @@
     bases = rotary_tables(np.arange(SECTIONS * HEADS) * PIECE)
     steps = rotary_tables(np.arange(PIECE))
     gain = norm_gain.reshape(1, D)
-    summed = layer(block_lists, hidden_in, gain, weight, w_out, bases + steps)
-    return (hidden_in.astype(jnp.float32) + summed).astype(jnp.bfloat16)
+    return layer(block_lists, hidden_in, gain, weight, w_out, bases + steps)
 
 
 def solution(mesh):

time: 133 us -> 131 us (0.985)
  the two profiles are of different devices: /device:TPU:7 before, /device:TPU:97 now
where the time goes in v8:
time: 131 us
  Pallas kernels  129 us (98%)
  local copies, waits for them, and re-layouts  2.09 us (2%)
    pallas_call x1, Pallas kernels, layer(): pl.pallas_call(layer_kernel, out_shape=jax.ShapeDtypeStruct((PIECE, D), j...  129 us

profile of v8, /device:TPU:97, one launch (start us, length us, event | category | flops | bytes accessed | tf_op | source)
XLA Modules:
  0.0 131.3 jit_solution(17465299863074729472)
XLA Ops:
  0.0 129.2 %layer.1 = bf16[192,2048]{1,0:T(8,128)(2,1)} custom-call(s32[6,12]{1,0:T(8,128)} %lists_here.1, bf16[192,2048]{1,0:T(8,128)(2,1)} %hidden_in.1, f32[1,2048]{1,0:T(1,128)} %bitcast.3, bf16[3,2048,128]{2,1,0:T(8,128)(2,1)} %bitcast.2, bf16[128,2048]{1,0:T(8,128)(2,1)} %shard.1, f32[128,128]{1,0:T(8,128)} %constant.8.clone.cos_b, ...), custom_call_target="tpu_custom_call" | custom-call | tf_op jit(solution)/shard_map/layer/pallas_call | solution.py:628
  129.2 2.1 %copy.11 = bf16[192,2048]{1,0:T(8,128)(2,1)} copy(bf16[192,2048]{1,0:T(8,128)(2,1)} %layer.1) | data formatting | bytes 1572864

commit v9 on v8

--- a/solution.py
+++ b/solution.py
@@ -29,7 +29,7 @@
 TOK = PIECE * HEADS
 STAGES = 6
 W_HALF = HD // 2
-W_PART = W_HALF // 2
+W_PART = W_HALF // 4
 BLOCKS = TOK // BLK
 MOVED = 3
 OUT_TILE = 256
@@ -42,7 +42,7 @@
     x_all, kv_all, q_ref, m_ref, acc_ref, o_ref, w_all, mix, w_two, q_two, kv_two,
     near_recv, far_recv, side_recv, copy_recv, x_send, v_send, v_recv, vp_send, vp_recv,
     rq_send, rk_send, rq_recv, rk_recv, z_send, z_recv, s_send, s_recv,
-    w_send, w_recv, wp_send, wp_recv, w_own, a_send, a_recv,
+    w_send, w_recv, wz_recv, wp_send, wp_recv, w_own, a_send, a_recv,
     lists, l_send, l_recv, l_own, m_send, m_recv,
 ):
     section = lax.axis_index("section")
@@ -63,6 +63,11 @@
     heavy = section >= SECTIONS // 2
     moved = (jnp.maximum(section, mate_section) - 1) // 2
 
+    own_hidden = pltpu.make_async_copy(hidden_in, hidden, in_sems.at[0])
+    own_weight = pltpu.make_async_copy(w_in, w_ref, in_sems.at[1])
+    own_hidden.start()
+    own_weight.start()
+
     barrier = pltpu.get_barrier_semaphore()
     for device in (z_up, z_down, partner):
         pl.semaphore_signal(barrier, inc=1, device_id=device, device_id_type=MESH)
@@ -80,10 +85,6 @@
         return carry
 
     lax.fori_loop(0, HEADS, greet_mates, 0)
-    own_hidden = pltpu.make_async_copy(hidden_in, hidden, in_sems.at[0])
-    own_weight = pltpu.make_async_copy(w_in, w_ref, in_sems.at[1])
-    own_hidden.start()
-    own_weight.start()
     own_hidden.wait()
     resid = hidden[...].astype(jnp.float32)
     spread = jnp.mean(resid * resid, axis=1, keepdims=True)
@@ -278,8 +279,10 @@
         project([stage], True)
         share(stage)
 
-    def w_rows(source, part):
-        return rows_of(source * HD + core * W_HALF + part * W_PART, W_PART)
+    parity = section // 2 % 2
+
+    def w_rows(source, part, side):
+        return rows_of(source * HD + core * W_HALF + side * 2 * W_PART + part * W_PART, W_PART)
 
     def line(part, step):
         if part == 0:
@@ -287,10 +290,10 @@
         return ((ypos + step) % 4) * 4 + xpos
 
     def w_copy(source, part, stage, target):
-        view = w_all.at[w_rows(source, part), :]
+        view = w_all.at[w_rows(source, part, parity), :]
         send(
             view,
-            w_all.at[w_rows(source, part), :],
+            view,
             w_send,
             w_recv.at[part, stage],
             {"section": section, "head": target},
@@ -400,24 +403,32 @@
     for index in range(2 * STAGES):
         arrived(kv_all, 4 * HALF * len(batch(index)), s_recv.at[index])
 
-    def w_to_partner(source, part):
-        rows = w_rows(source, part)
-        send(w_all.at[rows, :], w_all.at[rows, :], wp_send, wp_recv, partner)
-
-    def w_near_to_partner():
+    def w_group(part, step):
+        if step == 0:
+            return [line(part, other) for other in range(1, 4)]
+        if part == 0:
+            return [(ypos + 4 - step) % 4 * 4 + other for other in range(4)]
+        return [other * 4 + (xpos + 4 - step) % 4 for other in range(4)]
+
+    def w_to_partner(source, part, side):
+        view = w_all.at[w_rows(source, part, side), :]
+        send(view, view, wp_send, wp_recv, partner)
+
+    def w_spread(step):
         for part in range(2):
-            for step in range(1, 4):
-                w_to_partner(line(part, step), part)
-
-    def w_far_to_partner(step):
+            if step > 0:
+                arrived(w_all, 4 * W_PART, w_recv.at[part, step])
+            for source in w_group(part, step):
+                view = w_all.at[w_rows(source, part, parity), :]
+                send(view, view, w_send, wz_recv.at[part, step], z_down if part else z_up)
+                w_to_partner(source, part, parity)
+
+    def w_finish(step):
         for part in range(2):
-            arrived(w_all, 4 * W_PART, w_recv.at[part, step])
-            for other in range(4):
-                if part == 0:
-                    source = (ypos + 4 - step) % 4 * 4 + other
-                else:
-                    source = other * 4 + (xpos + 4 - step) % 4
-                w_to_partner(source, part)
+            sources = w_group(part, step)
+            arrived(w_all, len(sources) * W_PART, wz_recv.at[part, step])
+            for source in sources:
+                w_to_partner(source, part, 1 - parity)
 
     def copies_of(turn, own, phase):
         base = own % BLOCKS * BLK
@@ -568,19 +579,26 @@
             ).astype(jnp.bfloat16)
         deliver(turn, own)
 
-        @pl.when(turn == turns - 3)
+        @pl.when(turn == 0)
         def _():
-            w_near_to_partner()
+            w_spread(1)
+            w_spread(3)
+
+        @pl.when(turn == (turns - 1) // 3)
+        def _():
+            w_spread(2)
 
         @pl.when(turn == turns - 2)
         def _():
-            w_far_to_partner(1)
-            w_far_to_partner(3)
+            w_finish(0)
 
         return carry
 
+    w_spread(0)
     lax.fori_loop(0, turns, one_block, 0)
-    w_far_to_partner(2)
+    w_finish(1)
+    w_finish(3)
+    w_finish(2)
     arrived(w_all, (HEADS - 1) * W_HALF, wp_recv)
     pltpu.make_async_copy(mix, mix, a_recv).wait()
 
@@ -596,7 +614,7 @@
 
     lax.fori_loop(0, D // OUT_TILE, one_tile, 0)
 
-    arrived(w_all, 30 * W_PART, w_send)
+    arrived(w_all, 60 * W_PART, w_send)
     arrived(w_all, (HEADS - 1) * W_HALF, wp_send)
 
     def sent(turn, carry):
@@ -665,6 +683,7 @@
             dma((2 * STAGES,)),
             dma,
             dma((2, 4)),
+            dma((2, 4)),
             dma,
             dma,
             dma,

time: 131 us -> 134 us (1.023)
  the two profiles are of different devices: /device:TPU:97 before, /device:TPU:103 now
where the time goes in v9:
time: 134 us
  Pallas kernels  132 us (99%)
  local copies, waits for them, and re-layouts  2.09 us (2%)
    pallas_call x1, Pallas kernels, layer(): pl.pallas_call(layer_kernel, out_shape=jax.ShapeDtypeStruct((PIECE, D), j...  132 us

profile of v9, /device:TPU:103, one launch (start us, length us, event | category | flops | bytes accessed | tf_op | source)
XLA Modules:
  0.0 134.2 jit_solution(210784026669108550)
XLA Ops:
  0.0 132.1 %layer.1 = bf16[192,2048]{1,0:T(8,128)(2,1)} custom-call(s32[6,12]{1,0:T(8,128)} %lists_here.1, bf16[192,2048]{1,0:T(8,128)(2,1)} %hidden_in.1, f32[1,2048]{1,0:T(1,128)} %bitcast.3, bf16[3,2048,128]{2,1,0:T(8,128)(2,1)} %bitcast.2, bf16[128,2048]{1,0:T(8,128)(2,1)} %shard.1, f32[128,128]{1,0:T(8,128)} %constant.8.clone.cos_b, ...), custom_call_target="tpu_custom_call" | custom-call | tf_op jit(solution)/shard_map/layer/pallas_call | solution.py:646
  132.1 2.1 %copy.11 = bf16[192,2048]{1,0:T(8,128)(2,1)} copy(bf16[192,2048]{1,0:T(8,128)(2,1)} %layer.1) | data formatting | bytes 1572864

commit v10 on v8

--- a/solution.py
+++ b/solution.py
@@ -42,7 +42,7 @@
     x_all, kv_all, q_ref, m_ref, acc_ref, o_ref, w_all, mix, w_two, q_two, kv_two,
     near_recv, far_recv, side_recv, copy_recv, x_send, v_send, v_recv, vp_send, vp_recv,
     rq_send, rk_send, rq_recv, rk_recv, z_send, z_recv, s_send, s_recv,
-    w_send, w_recv, wp_send, wp_recv, w_own, a_send, a_recv,
+    w_send, w_recv, w_far, wp_send, wp_recv, w_own, a_send, a_recv,
     lists, l_send, l_recv, l_own, m_send, m_recv,
 ):
     section = lax.axis_index("section")
@@ -63,6 +63,11 @@
     heavy = section >= SECTIONS // 2
     moved = (jnp.maximum(section, mate_section) - 1) // 2
 
+    own_hidden = pltpu.make_async_copy(hidden_in, hidden, in_sems.at[0])
+    own_weight = pltpu.make_async_copy(w_in, w_ref, in_sems.at[1])
+    own_hidden.start()
+    own_weight.start()
+
     barrier = pltpu.get_barrier_semaphore()
     for device in (z_up, z_down, partner):
         pl.semaphore_signal(barrier, inc=1, device_id=device, device_id_type=MESH)
@@ -80,10 +85,6 @@
         return carry
 
     lax.fori_loop(0, HEADS, greet_mates, 0)
-    own_hidden = pltpu.make_async_copy(hidden_in, hidden, in_sems.at[0])
-    own_weight = pltpu.make_async_copy(w_in, w_ref, in_sems.at[1])
-    own_hidden.start()
-    own_weight.start()
     own_hidden.wait()
     resid = hidden[...].astype(jnp.float32)
     spread = jnp.mean(resid * resid, axis=1, keepdims=True)
@@ -278,36 +279,64 @@
         project([stage], True)
         share(stage)
 
-    def w_rows(source, part):
-        return rows_of(source * HD + core * W_HALF + part * W_PART, W_PART)
+    def w_rows(source, part, first, size):
+        return rows_of(source * HD + core * W_HALF + part * W_PART + first, size)
 
     def line(part, step):
         if part == 0:
             return ypos * 4 + (xpos + step) % 4
         return ((ypos + step) % 4) * 4 + xpos
 
-    def w_copy(source, part, stage, target):
-        view = w_all.at[w_rows(source, part), :]
-        send(
-            view,
-            w_all.at[w_rows(source, part), :],
-            w_send,
-            w_recv.at[part, stage],
-            {"section": section, "head": target},
-        )
-
-    def w_near():
-        own_rows.wait()
+    def w_copy(source, part, sems, stage, way, target, first=0, size=W_PART):
+        view = w_all.at[w_rows(source, part, first, size), :]
+        sem = sems.at[part, stage, way]
+        send(view, view, w_send, sem, {"section": section, "head": target})
+
+    def w_line(part, stage, step):
+        if stage == 0:
+            return [line(part, step)]
+        if part == 0:
+            return [(ypos + step) % 4 * 4 + other for other in range(4)]
+        return [other * 4 + (xpos + step) % 4 for other in range(4)]
+
+    def w_begin(stage):
         for part in range(2):
-            for step in range(1, 4):
-                w_copy(head, part, 0, line(part, step))
+            along = part if stage == 0 else 1 - part
+            for source in w_line(part, stage, 0):
+                w_copy(source, part, w_recv, stage, 0, line(along, 1))
+                w_copy(source, part, w_recv, stage, 1, line(along, 3))
+
+    def w_relay(stage):
+        count = 1 if stage == 0 else 4
+        for part in range(2):
+            along = part if stage == 0 else 1 - part
+            for way in range(2):
+                arrived(w_all, count * W_PART, w_recv.at[part, stage, way])
+                for source in w_line(part, stage, 3 - 2 * way):
+                    first = way * (W_PART // 2)
+                    target = line(along, 1 + 2 * way)
+                    w_copy(source, part, w_far, stage, way, target, first, W_PART // 2)
+
+    def w_complete(stage):
+        count = 1 if stage == 0 else 4
+        for part in range(2):
+            for way in range(2):
+                arrived(w_all, count * (W_PART // 2), w_far.at[part, stage, way])
+
+    def w_to_partner(stage, steps):
+        for part in range(2):
+            for step in steps:
+                for source in w_line(part, stage, step):
+                    view = w_all.at[w_rows(source, part, 0, W_PART), :]
+                    send(view, view, wp_send, wp_recv, partner)
 
     def last_stage(stage):
         for way in range(2):
             arrived(x_all, HALF, copy_recv.at[way, stage - 4])
         arrived(x_all, HALF, side_recv.at[1, stage - 4])
         if stage == 5:
-            w_near()
+            own_rows.wait()
+            w_begin(0)
         project([stage], True)
         share(stage)
         project([stage], False, (1, 2))
@@ -366,13 +395,11 @@
     project([4, 5], False, (0,))
     queries_home(4)
     queries_home(5)
+    w_relay(0)
     relay_near(4)
     bring(4)
-    for part in range(2):
-        arrived(w_all, 3 * W_PART, w_recv.at[part, 0])
-        for step in range(1, 4):
-            for other in range(4):
-                w_copy(line(part, other), part, step, line(1 - part, step))
+    w_complete(0)
+    w_begin(1)
     relay_near(5)
     relay_far(STAGES + 3)
     relay_far(4)
@@ -399,25 +426,6 @@
     relay_far(STAGES + 5)
     for index in range(2 * STAGES):
         arrived(kv_all, 4 * HALF * len(batch(index)), s_recv.at[index])
-
-    def w_to_partner(source, part):
-        rows = w_rows(source, part)
-        send(w_all.at[rows, :], w_all.at[rows, :], wp_send, wp_recv, partner)
-
-    def w_near_to_partner():
-        for part in range(2):
-            for step in range(1, 4):
-                w_to_partner(line(part, step), part)
-
-    def w_far_to_partner(step):
-        for part in range(2):
-            arrived(w_all, 4 * W_PART, w_recv.at[part, step])
-            for other in range(4):
-                if part == 0:
-                    source = (ypos + 4 - step) % 4 * 4 + other
-                else:
-                    source = other * 4 + (xpos + 4 - step) % 4
-                w_to_partner(source, part)
 
     def copies_of(turn, own, phase):
         base = own % BLOCKS * BLK
@@ -568,19 +576,20 @@
             ).astype(jnp.bfloat16)
         deliver(turn, own)
 
-        @pl.when(turn == turns - 3)
+        @pl.when(turn == (turns - 1) // 3)
         def _():
-            w_near_to_partner()
+            w_relay(1)
+            w_to_partner(0, (1, 2, 3))
+            w_to_partner(1, (1, 3))
 
         @pl.when(turn == turns - 2)
         def _():
-            w_far_to_partner(1)
-            w_far_to_partner(3)
+            w_complete(1)
+            w_to_partner(1, (2,))
 
         return carry
 
     lax.fori_loop(0, turns, one_block, 0)
-    w_far_to_partner(2)
     arrived(w_all, (HEADS - 1) * W_HALF, wp_recv)
     pltpu.make_async_copy(mix, mix, a_recv).wait()
 
@@ -664,7 +673,8 @@
             dma,
             dma((2 * STAGES,)),
             dma,
-            dma((2, 4)),
+            dma((2, 2, 2)),
+            dma((2, 2, 2)),
             dma,
             dma,
             dma,

time: 131 us -> 133 us (1.015)
  the two profiles are of different devices: /device:TPU:97 before, /device:TPU:1 now
where the time goes in v10:
time: 133 us
  Pallas kernels  131 us (98%)
  local copies, waits for them, and re-layouts  2.09 us (2%)
    pallas_call x1, Pallas kernels, layer(): pl.pallas_call(layer_kernel, out_shape=jax.ShapeDtypeStruct((PIECE, D), j...  131 us

profile of v10, /device:TPU:1, one launch (start us, length us, event | category | flops | bytes accessed | tf_op | source)
XLA Modules:
  0.0 133.1 jit_solution(11040744615941060288)
XLA Ops:
  0.0 131.0 %layer.1 = bf16[192,2048]{1,0:T(8,128)(2,1)} custom-call(s32[6,12]{1,0:T(8,128)} %lists_here.1, bf16[192,2048]{1,0:T(8,128)(2,1)} %hidden_in.1, f32[1,2048]{1,0:T(1,128)} %bitcast.3, bf16[3,2048,128]{2,1,0:T(8,128)(2,1)} %bitcast.2, bf16[128,2048]{1,0:T(8,128)(2,1)} %shard.1, f32[128,128]{1,0:T(8,128)} %constant.8.clone.cos_b, ...), custom_call_target="tpu_custom_call" | custom-call | tf_op jit(solution)/shard_map/layer/pallas_call | solution.py:637
  131.1 2.1 %copy.11 = bf16[192,2048]{1,0:T(8,128)(2,1)} copy(bf16[192,2048]{1,0:T(8,128)(2,1)} %layer.1) | data formatting | bytes 1572864

commit v11 on v10

--- a/solution.py
+++ b/solution.py
@@ -32,6 +32,7 @@
 W_PART = W_HALF // 2
 BLOCKS = TOK // BLK
 MOVED = 3
+AHEAD = 3
 OUT_TILE = 256
 MESH = pl.DeviceIdType.MESH
 
@@ -62,6 +63,8 @@
     mate = {"section": mate_section, "head": head}
     heavy = section >= SECTIONS // 2
     moved = (jnp.maximum(section, mate_section) - 1) // 2
+    shift = 1 - jnp.maximum(section, mate_section) % 2
+
 
     own_hidden = pltpu.make_async_copy(hidden_in, hidden, in_sems.at[0])
     own_weight = pltpu.make_async_copy(w_in, w_ref, in_sems.at[1])
@@ -412,7 +415,7 @@
         @pl.when(heavy & (block < moved))
         def _(block=block):
             send(
-                q_ref.at[pl.ds(block * BLK, BLK), :],
+                q_ref.at[rows_of((2 * block + shift) * BLK, BLK), :],
                 q_ref.at[pl.ds(TOK + block * BLK, BLK), :],
                 m_send.at[block],
                 m_recv.at[block],
@@ -486,24 +489,27 @@
     kept = BLOCKS - given
 
     def block_of(turn):
-        away = turn >= kept
-        here = given + (turn + head) % kept
-        there = (jnp.maximum(turn - kept, 0) + head) % jnp.maximum(taken, 1)
-        row = jnp.where(away, there, here)
+        away = (turn >= AHEAD) & (turn < AHEAD + taken)
+        place = jnp.where(turn < AHEAD, turn, turn - taken)
+        place = (place + head) % kept
+        here = jnp.where(place < given, 2 * place + 1 - shift, place + given)
+        there = (jnp.maximum(turn - AHEAD, 0) + head) % jnp.maximum(taken, 1)
+        row = jnp.where(away, 2 * there + shift, here)
         side = jnp.where(away, 1, 0)
         own = jnp.where(away, mate_section, section) * BLOCKS + row
-        return own, side, row, row * BLK + side * TOK
+        base = jnp.where(away, TOK + there * BLK, row * BLK)
+        return own, side, row, base, away, there
 
     ones = jnp.ones((BLK, HD), jnp.bfloat16)
 
     def one_block(turn, carry):
-        own, side, block, base = block_of(turn)
+        own, side, block, base, away, there = block_of(turn)
         base = pl.multiple_of(base, BLK)
         landing = pl.multiple_of(turn * BLK, BLK)
 
-        @pl.when(turn >= kept)
+        @pl.when(away)
         def _():
-            arrived(q_ref, BLK, m_recv.at[block])
+            arrived(q_ref, BLK, m_recv.at[there])
 
         others = (own * (KSEL - 1)) // (NBLK - 1)
         spare = others % GROUP

time: 133 us -> 125 us (0.940)
  the two profiles are of different devices: /device:TPU:1 before, /device:TPU:8 now
where the time goes in v11:
time: 125 us
  Pallas kernels  123 us (98%)
  local copies, waits for them, and re-layouts  2.09 us (2%)
    pallas_call x1, Pallas kernels, layer(): pl.pallas_call(layer_kernel, out_shape=jax.ShapeDtypeStruct((PIECE, D), j...  123 us

profile of v11, /device:TPU:8, one launch (start us, length us, event | category | flops | bytes accessed | tf_op | source)
XLA Modules:
  0.0 124.7 jit_solution(4409216419650948354)
XLA Ops:
  0.0 122.6 %layer.1 = bf16[192,2048]{1,0:T(8,128)(2,1)} custom-call(s32[6,12]{1,0:T(8,128)} %lists_here.1, bf16[192,2048]{1,0:T(8,128)(2,1)} %hidden_in.1, f32[1,2048]{1,0:T(1,128)} %bitcast.3, bf16[3,2048,128]{2,1,0:T(8,128)(2,1)} %bitcast.2, bf16[128,2048]{1,0:T(8,128)(2,1)} %shard.1, f32[128,128]{1,0:T(8,128)} %constant.8.clone.cos_b, ...), custom_call_target="tpu_custom_call" | custom-call | tf_op jit(solution)/shard_map/layer/pallas_call | solution.py:643
  122.6 2.1 %copy.11 = bf16[192,2048]{1,0:T(8,128)(2,1)} copy(bf16[192,2048]{1,0:T(8,128)(2,1)} %layer.1) | data formatting | bytes 1572864

commit v12 on v11

--- a/solution.py
+++ b/solution.py
@@ -33,7 +33,7 @@
 BLOCKS = TOK // BLK
 MOVED = 3
 AHEAD = 3
-OUT_TILE = 256
+OUT_TILE = 512
 MESH = pl.DeviceIdType.MESH
 
 
@@ -62,7 +62,7 @@
     mate_section = SECTIONS - 1 - section
     mate = {"section": mate_section, "head": head}
     heavy = section >= SECTIONS // 2
-    moved = (jnp.maximum(section, mate_section) - 1) // 2
+    moved = (jnp.maximum(section, mate_section) - 2) // 2
     shift = 1 - jnp.maximum(section, mate_section) % 2
 
 

time: 125 us -> 120 us (0.960)
  the two profiles are of different devices: /device:TPU:8 before, /device:TPU:33 now
where the time goes in v12:
time: 120 us
  Pallas kernels  118 us (98%)
  local copies, waits for them, and re-layouts  2.09 us (2%)
    pallas_call x1, Pallas kernels, layer(): pl.pallas_call(layer_kernel, out_shape=jax.ShapeDtypeStruct((PIECE, D), j...  118 us

profile of v12, /device:TPU:33, one launch (start us, length us, event | category | flops | bytes accessed | tf_op | source)
XLA Modules:
  0.0 119.8 jit_solution(3397315170470735080)
XLA Ops:
  0.0 117.7 %layer.1 = bf16[192,2048]{1,0:T(8,128)(2,1)} custom-call(s32[6,12]{1,0:T(8,128)} %lists_here.1, bf16[192,2048]{1,0:T(8,128)(2,1)} %hidden_in.1, f32[1,2048]{1,0:T(1,128)} %bitcast.3, bf16[3,2048,128]{2,1,0:T(8,128)(2,1)} %bitcast.2, bf16[128,2048]{1,0:T(8,128)(2,1)} %shard.1, f32[128,128]{1,0:T(8,128)} %constant.8.clone.cos_b, ...), custom_call_target="tpu_custom_call" | custom-call | tf_op jit(solution)/shard_map/layer/pallas_call | solution.py:643
  117.7 2.1 %copy.11 = bf16[192,2048]{1,0:T(8,128)(2,1)} copy(bf16[192,2048]{1,0:T(8,128)(2,1)} %layer.1) | data formatting | bytes 1572864
